TPU v7x, 32 devices: a whole 2x2x4 slice. The times are simulated.
32 devices in a mesh: dp: 8 (over y, x, core), tensor: 4 (over z).
Axes of the slice: x: 2, y: 2, z: 4, core: 2. Of those that a mesh axis runs over, the one named last changes fastest.
Arguments:
- tokens: bfloat16 [2, 8192, 1536], P(None, ('dp', 'tensor')), may hold values from -6 to 6
- cotangent: bfloat16 [2, 8192, 1536], P(None, ('dp', 'tensor')), may hold values from -6 to 6
- segment_ids: int32 [2, 8192], P(None, 'dp'), may hold values from 0 to 1, as said below
- slot_mask: int32 [2, 8192], P(None, 'dp'), may hold values from 0 to 1, as said below
- attention_gain: float32 [1536], replicated, may hold values from 0.5 to 1.5
- query_weight: bfloat16 [1536, 1536], P('dp', 'tensor'), may hold values from -0.15625 to 0.15625
- key_weight: bfloat16 [1536, 1536], P('dp', 'tensor'), may hold values from -0.15625 to 0.15625
- value_weight: bfloat16 [1536, 1536], P('dp', 'tensor'), may hold values from -0.15625 to 0.15625
- forget_weight: bfloat16 [1536, 24], P('dp', 'tensor'), may hold values from -0.15625 to 0.15625
- forget_bias: float32 [24], replicated, may hold values from 1 to 8
- output_weight: bfloat16 [1536, 1536], P(('tensor', 'dp')), may hold values from -0.625 to 0.625
- swiglu_gain: float32 [1536], replicated, may hold values from 0.5 to 1.5
- gate_weight: bfloat16 [1536, 4096], P('dp', 'tensor'), may hold values from -0.15625 to 0.15625
- up_weight: bfloat16 [1536, 4096], P('dp', 'tensor'), may hold values from -0.15625 to 0.15625
- down_weight: bfloat16 [4096, 1536], P(('tensor', 'dp')), may hold values from -0.1875 to 0.1875
Outputs:
- layer_out: bfloat16 [2, 8192, 1536], P(None, ('dp', 'tensor'))
- grad_tokens: float32 [2, 8192, 1536], P(None, ('dp', 'tensor'))
- grad_attention_gain: float32 [1536], replicated
- grad_query: float32 [1536, 1536], P('dp', 'tensor')
- grad_key: float32 [1536, 1536], P('dp', 'tensor')
- grad_value: float32 [1536, 1536], P('dp', 'tensor')
- grad_forget: float32 [1536, 24], P('dp', 'tensor')
- grad_forget_bias: float32 [24], replicated
- grad_output: float32 [1536, 1536], P(('tensor', 'dp'))
- grad_swiglu_gain: float32 [1536], replicated
- grad_gate: float32 [1536, 4096], P('dp', 'tensor')
- grad_up: float32 [1536, 4096], P('dp', 'tensor')
- grad_down: float32 [4096, 1536], P(('tensor', 'dp'))
Inputs may be any that keep to these rules, and one draw needn't show every extreme that they name: `segment_ids`: within each aligned block of 1024 slots the ids start at 0 and never fall, and a block holds at most 2 sequences; every sequence lies in one block; the first block of every micro-batch holds one sequence. `slot_mask`: padding slots stand at the end of an aligned block of 1024 slots.
All inputs are finite; a program needn't handle non-finite values.
Results may differ from a plain program's by a relative error of at most 0.019.
Values may be sent and summed in bfloat16 or wider, within the bound.
No kernel may reach another device: no remote copies, remote signals or barrier semaphores. Data moves between devices by JAX's collectives and lax.ppermute only.
A program may use at most 168 MiB of HBM per device.

v0:
```python
import jax
import jax.numpy as jnp
from jax import lax
from jax.sharding import PartitionSpec as P

EPS = 1e-05
NEGATIVE = -1e30


def rms_forward(rows, gain):
    inverse = lax.rsqrt(jnp.mean(rows * rows, axis=-1, keepdims=True) + EPS)
    return (rows * inverse * gain, inverse)


def rms_backward(rows, inverse, gain, upstream):
    scaled = upstream * gain
    grad_rows = inverse * scaled - rows * inverse**3 * jnp.mean(
        scaled * rows, axis=-1, keepdims=True
    )
    grad_gain = jnp.sum(upstream * rows * inverse, axis=0)
    return (grad_rows, grad_gain)


def contract_first(left, right):
    return lax.dot_general(
        left, right, (((0,), (0,)), ((), ())), preferred_element_type=jnp.float32
    )


def contract_last(left, right):
    return lax.dot_general(
        left, right, (((1,), (1,)), ((), ())), preferred_element_type=jnp.float32
    )


def allowed_block(segment, present, first, size):
    length = segment.shape[0]
    places = jnp.arange(length, dtype=jnp.int32)
    query_places = first + jnp.arange(size, dtype=jnp.int32)
    query_segment = segment[first : first + size]
    allowed = (places[None, :] <= query_places[:, None]) & (
        query_segment[:, None] == segment[None, :]
    )
    return allowed & ((present[None, :] == 1) | (places[None, :] == query_places[:, None]))


def block_scores(query_block, keys_all, decay, first, size, allowed, scale):
    raw = (
        jnp.einsum("qhd,khd->hqk", query_block, keys_all, preferred_element_type=jnp.float32)
        * scale
    )
    raw = raw + decay[:, first : first + size, None] - decay[:, None, :]
    return jnp.where(allowed[None], raw, NEGATIVE)


def attention_forward(queries, keys_all, values_all, decay, segment, present):
    length = queries.shape[0]
    scale = queries.shape[2] ** (-0.5)
    block = min(512, length)
    mixed_blocks = []
    total_blocks = []
    for first in range(0, length, block):
        allowed = allowed_block(segment, present, first, block)
        scores = block_scores(
            queries[first : first + block], keys_all, decay, first, block, allowed, scale
        )
        highest = jnp.max(scores, axis=-1, keepdims=True)
        expo = jnp.exp(scores - highest)
        denominator = jnp.sum(expo, axis=-1, keepdims=True)
        probs = (expo / denominator).astype(jnp.bfloat16)
        mixed_blocks.append(
            jnp.einsum(
                "hqk,khd->qhd", probs, values_all, preferred_element_type=jnp.float32
            ).astype(jnp.bfloat16)
        )
        total_blocks.append((highest + jnp.log(denominator))[:, :, 0])
    return (jnp.concatenate(mixed_blocks, axis=0), jnp.concatenate(total_blocks, axis=1))


def attention_backward(
    queries, keys_all, values_all, decay, log_total, grad_mixed, segment, present
):
    length = queries.shape[0]
    scale = queries.shape[2] ** (-0.5)
    block = min(512, length)
    grad_keys = jnp.zeros(keys_all.shape, jnp.float32)
    grad_values = jnp.zeros(values_all.shape, jnp.float32)
    grad_decay = jnp.zeros(decay.shape, jnp.float32)
    query_grads = []
    for first in range(0, length, block):
        allowed = allowed_block(segment, present, first, block)
        query_block = queries[first : first + block]
        grad_block = grad_mixed[first : first + block]
        scores = block_scores(query_block, keys_all, decay, first, block, allowed, scale)
        probs = jnp.exp(scores - log_total[:, first : first + block, None])
        grad_values = grad_values + jnp.einsum(
            "hqk,qhd->khd",
            probs.astype(jnp.bfloat16),
            grad_block,
            preferred_element_type=jnp.float32,
        )
        grad_probs = jnp.einsum(
            "qhd,khd->hqk", grad_block, values_all, preferred_element_type=jnp.float32
        )
        grad_scores = probs * (grad_probs - jnp.sum(probs * grad_probs, axis=-1, keepdims=True))
        grad_low = grad_scores.astype(jnp.bfloat16)
        query_grads.append(
            (
                jnp.einsum("hqk,khd->qhd", grad_low, keys_all, preferred_element_type=jnp.float32)
                * scale
            ).astype(jnp.bfloat16)
        )
        grad_keys = (
            grad_keys
            + jnp.einsum("hqk,qhd->khd", grad_low, query_block, preferred_element_type=jnp.float32)
            * scale
        )
        as_float = grad_low.astype(jnp.float32)
        grad_decay = grad_decay.at[:, first : first + block].add(jnp.sum(as_float, axis=-1))
        grad_decay = grad_decay - jnp.sum(as_float, axis=1)
    return (
        jnp.concatenate(query_grads, axis=0),
        grad_keys.astype(jnp.bfloat16),
        grad_values.astype(jnp.bfloat16),
        grad_decay,
    )


def body(
    tokens,
    cotangent,
    segment_ids,
    slot_mask,
    attention_gain,
    query_weight,
    key_weight,
    value_weight,
    forget_weight,
    forget_bias,
    output_weight,
    swiglu_gain,
    gate_weight,
    up_weight,
    down_weight,
):
    batches = tokens.shape[0]
    heads_here = forget_weight.shape[1]
    tensor_rank = lax.axis_index("tensor")
    bias_here = lax.dynamic_slice_in_dim(forget_bias, tensor_rank * heads_here, heads_here)
    shards = (
        query_weight,
        key_weight,
        value_weight,
        forget_weight,
        output_weight,
        gate_weight,
        up_weight,
        down_weight,
    )
    saved = []
    outputs = []
    for batch in range(batches):
        full = (
            lax.all_gather(shards[0], "dp", axis=0, tiled=True),
            lax.all_gather(shards[1], "dp", axis=0, tiled=True),
            lax.all_gather(shards[2], "dp", axis=0, tiled=True),
            lax.all_gather(shards[3], "dp", axis=0, tiled=True),
            lax.all_gather(shards[4], "dp", axis=0, tiled=True),
            lax.all_gather(shards[5], "dp", axis=0, tiled=True),
            lax.all_gather(shards[6], "dp", axis=0, tiled=True),
            lax.all_gather(shards[7], "dp", axis=0, tiled=True),
        )
        (
            full_query,
            full_key,
            full_value,
            full_forget,
            full_output,
            full_gate,
            full_up,
            full_down,
        ) = full
        head_size = full_query.shape[1] // heads_here
        rows = tokens[batch].astype(jnp.float32)
        normed, inverse_one = rms_forward(rows, attention_gain)
        normed_all = lax.all_gather(normed.astype(jnp.bfloat16), "tensor", axis=0, tiled=True)
        length = normed_all.shape[0]
        queries = jnp.dot(normed_all, full_query, preferred_element_type=jnp.float32).astype(
            jnp.bfloat16
        )
        keys_all = jnp.dot(normed_all, full_key, preferred_element_type=jnp.float32).astype(
            jnp.bfloat16
        )
        values_all = jnp.dot(normed_all, full_value, preferred_element_type=jnp.float32).astype(
            jnp.bfloat16
        )
        queries = queries.reshape(length, heads_here, head_size)
        keys_all = keys_all.reshape(length, heads_here, head_size)
        values_all = values_all.reshape(length, heads_here, head_size)
        logits = jnp.dot(normed_all, full_forget, preferred_element_type=jnp.float32) + bias_here
        decay = jnp.cumsum(jax.nn.log_sigmoid(logits), axis=0).T
        mixed, log_total = attention_forward(
            queries, keys_all, values_all, decay, segment_ids[batch], slot_mask[batch]
        )
        mixed_flat = mixed.reshape(length, heads_here * head_size)
        attention_rows = lax.psum_scatter(
            jnp.dot(mixed_flat, full_output, preferred_element_type=jnp.float32),
            "tensor",
            scatter_dimension=0,
            tiled=True,
        )
        hidden_state = rows + attention_rows
        normed_two, inverse_two = rms_forward(hidden_state, swiglu_gain)
        swiglu_input = lax.all_gather(normed_two.astype(jnp.bfloat16), "tensor", axis=0, tiled=True)
        gate = jnp.dot(swiglu_input, full_gate, preferred_element_type=jnp.float32)
        upper = jnp.dot(swiglu_input, full_up, preferred_element_type=jnp.float32)
        inner = (jax.nn.silu(gate) * upper).astype(jnp.bfloat16)
        swiglu_out = lax.psum_scatter(
            jnp.dot(inner, full_down, preferred_element_type=jnp.float32).astype(jnp.bfloat16),
            "tensor",
            scatter_dimension=0,
            tiled=True,
        ).astype(jnp.float32)
        outputs.append((hidden_state + swiglu_out).astype(jnp.bfloat16))
        saved.append(
            (
                rows,
                inverse_one,
                normed_all,
                queries,
                keys_all,
                values_all,
                logits,
                decay,
                log_total,
                mixed_flat,
                hidden_state,
                inverse_two,
                swiglu_input,
                gate,
                upper,
                inner,
            )
        )
    accumulated = tuple((jnp.zeros(piece.shape, jnp.float32) for piece in shards))
    gain_one = jnp.zeros(attention_gain.shape, jnp.float32)
    gain_two = jnp.zeros(swiglu_gain.shape, jnp.float32)
    bias_grad = jnp.zeros((heads_here,), jnp.float32)
    grad_rows_list = [None] * batches
    for batch in reversed(range(batches)):
        (
            rows,
            inverse_one,
            normed_all,
            queries,
            keys_all,
            values_all,
            logits,
            decay,
            log_total,
            mixed_flat,
            hidden_state,
            inverse_two,
            swiglu_input,
            gate,
            upper,
            inner,
        ) = saved[batch]
        full = (
            lax.all_gather(shards[0], "dp", axis=0, tiled=True),
            lax.all_gather(shards[1], "dp", axis=0, tiled=True),
            lax.all_gather(shards[2], "dp", axis=0, tiled=True),
            lax.all_gather(shards[3], "dp", axis=0, tiled=True),
            lax.all_gather(shards[4], "dp", axis=0, tiled=True),
            lax.all_gather(shards[5], "dp", axis=0, tiled=True),
            lax.all_gather(shards[6], "dp", axis=0, tiled=True),
            lax.all_gather(shards[7], "dp", axis=0, tiled=True),
        )
        (
            full_query,
            full_key,
            full_value,
            full_forget,
            full_output,
            full_gate,
            full_up,
            full_down,
        ) = full
        length = normed_all.shape[0]
        upstream = cotangent[batch]
        upstream_all = lax.all_gather(upstream, "tensor", axis=0, tiled=True)
        grad_inner = contract_last(upstream_all, full_down)
        sigmoid_gate = jax.nn.sigmoid(gate)
        grad_gate_in = (
            grad_inner * upper * sigmoid_gate * (1.0 + gate * (1.0 - sigmoid_gate))
        ).astype(jnp.bfloat16)
        grad_upper = (grad_inner * gate * sigmoid_gate).astype(jnp.bfloat16)
        down_grad = contract_first(inner, upstream_all)
        gate_grad = contract_first(swiglu_input, grad_gate_in)
        up_grad = contract_first(swiglu_input, grad_upper)
        grad_normed_two = lax.psum_scatter(
            contract_last(grad_gate_in, full_gate) + contract_last(grad_upper, full_up),
            "tensor",
            scatter_dimension=0,
            tiled=True,
        )
        hidden_part, gain_two_part = rms_backward(
            hidden_state, inverse_two, swiglu_gain, grad_normed_two
        )
        grad_hidden = upstream.astype(jnp.float32) + hidden_part
        branch_all = lax.all_gather(grad_hidden.astype(jnp.bfloat16), "tensor", axis=0, tiled=True)
        grad_mixed = contract_last(branch_all, full_output).astype(jnp.bfloat16)
        output_grad = contract_first(mixed_flat, branch_all)
        grad_queries, grad_keys, grad_values, grad_decay = attention_backward(
            queries,
            keys_all,
            values_all,
            decay,
            log_total,
            grad_mixed.reshape(queries.shape),
            segment_ids[batch],
            slot_mask[batch],
        )
        carried = jnp.flip(jnp.cumsum(jnp.flip(grad_decay.T, 0), axis=0), 0)
        grad_logits = (carried * jax.nn.sigmoid(-logits)).astype(jnp.bfloat16)
        grad_queries = grad_queries.reshape(length, -1)
        grad_keys = grad_keys.reshape(length, -1)
        grad_values = grad_values.reshape(length, -1)
        query_grad = contract_first(normed_all, grad_queries)
        key_grad = contract_first(normed_all, grad_keys)
        value_grad = contract_first(normed_all, grad_values)
        forget_grad = contract_first(normed_all, grad_logits)
        bias_grad = bias_grad + jnp.sum(grad_logits.astype(jnp.float32), axis=0)
        total = contract_last(grad_queries, full_query)
        total = total + contract_last(grad_keys, full_key)
        total = total + contract_last(grad_values, full_value)
        grad_normed = lax.psum_scatter(
            (total + contract_last(grad_logits, full_forget)).astype(jnp.bfloat16),
            "tensor",
            scatter_dimension=0,
            tiled=True,
        ).astype(jnp.float32)
        rows_part, gain_one_part = rms_backward(rows, inverse_one, attention_gain, grad_normed)
        grad_rows_list[batch] = grad_hidden + rows_part
        gain_one = gain_one + gain_one_part
        gain_two = gain_two + gain_two_part
        terms = (
            query_grad,
            key_grad,
            value_grad,
            forget_grad,
            output_grad,
            gate_grad,
            up_grad,
            down_grad,
        )
        pieces = (
            lax.psum_scatter(
                terms[0].astype(jnp.bfloat16), "dp", scatter_dimension=0, tiled=True
            ).astype(jnp.float32),
            lax.psum_scatter(
                terms[1].astype(jnp.bfloat16), "dp", scatter_dimension=0, tiled=True
            ).astype(jnp.float32),
            lax.psum_scatter(
                terms[2].astype(jnp.bfloat16), "dp", scatter_dimension=0, tiled=True
            ).astype(jnp.float32),
            lax.psum_scatter(
                terms[3].astype(jnp.bfloat16), "dp", scatter_dimension=0, tiled=True
            ).astype(jnp.float32),
            lax.psum_scatter(
                terms[4].astype(jnp.bfloat16), "dp", scatter_dimension=0, tiled=True
            ).astype(jnp.float32),
            lax.psum_scatter(
                terms[5].astype(jnp.bfloat16), "dp", scatter_dimension=0, tiled=True
            ).astype(jnp.float32),
            lax.psum_scatter(
                terms[6].astype(jnp.bfloat16), "dp", scatter_dimension=0, tiled=True
            ).astype(jnp.float32),
            lax.psum_scatter(
                terms[7].astype(jnp.bfloat16), "dp", scatter_dimension=0, tiled=True
            ).astype(jnp.float32),
        )
        accumulated = tuple((held + piece for held, piece in zip(accumulated, pieces)))
    bias_full = lax.dynamic_update_slice_in_dim(
        jnp.zeros(forget_bias.shape, jnp.float32), bias_grad, tensor_rank * heads_here, 0
    )
    gain_one, gain_two, bias_full = lax.psum((gain_one, gain_two, bias_full), ("dp", "tensor"))
    (
        query_total,
        key_total,
        value_total,
        forget_total,
        output_total,
        gate_total,
        up_total,
        down_total,
    ) = accumulated
    return (
        jnp.stack(outputs),
        jnp.stack(grad_rows_list),
        gain_one,
        query_total,
        key_total,
        value_total,
        forget_total,
        bias_full,
        output_total,
        gain_two,
        gate_total,
        up_total,
        down_total,
    )


def solution(mesh):
    return jax.shard_map(
        body,
        mesh=mesh,
        in_specs=(
            P(None, ("dp", "tensor"), None),
            P(None, ("dp", "tensor"), None),
            P(None, "dp"),
            P(None, "dp"),
            P(),
            P("dp", "tensor"),
            P("dp", "tensor"),
            P("dp", "tensor"),
            P("dp", "tensor"),
            P(),
            P(("tensor", "dp"), None),
            P(),
            P("dp", "tensor"),
            P("dp", "tensor"),
            P(("tensor", "dp"), None),
        ),
        out_specs=(
            P(None, ("dp", "tensor"), None),
            P(None, ("dp", "tensor"), None),
            P(),
            P("dp", "tensor"),
            P("dp", "tensor"),
            P("dp", "tensor"),
            P("dp", "tensor"),
            P(),
            P(("tensor", "dp"), None),
            P(),
            P("dp", "tensor"),
            P("dp", "tensor"),
            P(("tensor", "dp"), None),
        ),
        check_vma=False,
    )
```

profile of v0, /device:TPU:9, one launch (start us, length us, event | category | flops | bytes accessed | tf_op | source)
XLA Modules:
  0.0 2220.1 jit_solution(8335198308266095401)
XLA Ops:
  18.2 9.6 all-gather.2
  30.6 44.8 %all-gather.19.cloned.1.call-done = bf16[1024,1536]{1,0:T(8,128)(2,1)} async-done(((bf16[256,1536]{1,0:T(8,128)(2,1)}), bf16[1024,1536]{1,0:T(8,128)(2,1)}) %all-gather.19.cloned.1.call-update) | async-done | bytes 3145744 | tf_op jit(solution)/shard_map/all_gather | solution.py:186
  82.3 20.5 all-gather.23.cloned.1.call-done
  106.3 22.3 %all-gather.25.cloned.1.call-done = bf16[1536,384]{1,0:T(8,128)(2,1)} async-done(((bf16[192,384]{1,0:T(8,128)(2,1)}), bf16[1536,384]{1,0:T(8,128)(2,1)}) %all-gather.25.cloned.1.call-update) | async-done | bytes 1179664 | tf_op jit(solution)/shard_map/all_gather | solution.py:165
  146.3 8.0 all-gather.21.cloned.1.call-done
  171.9 8.1 all-gather.27.cloned.1.call-done
  189.0 53.6 %all-gather.37.cloned.1.call-done = bf16[1024,1536]{1,0:T(8,128)(2,1)} async-done(((bf16[256,1536]{1,0:T(8,128)(2,1)}), bf16[1024,1536]{1,0:T(8,128)(2,1)}) %all-gather.37.cloned.1.call-update) | async-done | bytes 3145744 | tf_op jit(solution)/shard_map/all_gather | solution.py:186
  264.5 13.8 fusion.2
  291.4 65.4 %reduce-scatter.29.cloned.1.call-done = f32[256,1536]{1,0:T(8,128)} async-done(((f32[1024,1536]{1,0:T(8,128)}), f32[256,1536]{1,0:T(8,128)}) %reduce-scatter.29.cloned.1.call-update) | async-done | bytes 1572880 | tf_op jit(solution)/shard_map/reduce_scatter | solution.py:206
  356.8 113.6 %reduce-scatter.33.cloned.1.call-done = f32[256,1536]{1,0:T(8,128)} async-done(((f32[1024,1536]{1,0:T(8,128)}), f32[256,1536]{1,0:T(8,128)}) %reduce-scatter.33.cloned.1.call-update) | async-done | bytes 1572880 | tf_op jit(solution)/shard_map/reduce_scatter | solution.py:206
  477.9 27.7 %all-gather.33.cloned.1.call-done = bf16[1536,1024]{1,0:T(8,128)(2,1)} async-done(((bf16[192,1024]{1,0:T(8,128)(2,1)}), bf16[1536,1024]{1,0:T(8,128)(2,1)}) %all-gather.33.cloned.1.call-update) | async-done | bytes 3145744 | tf_op jit(solution)/shard_map/all_gather | solution.py:170
  505.5 62.5 %all-gather.29.cloned.1.call-done = bf16[1024,1536]{1,0:T(8,128)(2,1)} async-done(((bf16[256,1536]{1,0:T(8,128)(2,1)}), bf16[1024,1536]{1,0:T(8,128)(2,1)}) %all-gather.29.cloned.1.call-update) | async-done | bytes 3145744 | tf_op jit(solution)/shard_map/all_gather | solution.py:214
  568.1 8.2 fusion.117
  576.3 27.4 %all-gather.31.cloned.1.call-done = bf16[1536,1024]{1,0:T(8,128)(2,1)} async-done(((bf16[192,1024]{1,0:T(8,128)(2,1)}), bf16[1536,1024]{1,0:T(8,128)(2,1)}) %all-gather.31.cloned.1.call-update) | async-done | bytes 3145744 | tf_op jit(solution)/shard_map/all_gather | solution.py:169
  603.7 8.2 fusion.116
  612.0 54.3 %all-gather.45.cloned.1.call-done = bf16[1,1024,1536]{2,1,0:T(8,128)(2,1)} async-done(((bf16[1,256,1536]{2,1,0:T(8,128)(2,1)}), bf16[1,1024,1536]{2,1,0:T(8,128)(2,1)}) %all-gather.45.cloned.1.call-update) | async-done | bytes 3145744 | tf_op jit(solution)/shard_map/all_gather | solution.py:291
  666.3 35.7 %all-gather.35.cloned.1.call-done = bf16[1024,1536]{1,0:T(8,128)(2,1)} async-done(((bf16[128,1536]{1,0:T(8,128)(2,1)}), bf16[1024,1536]{1,0:T(8,128)(2,1)}) %all-gather.35.cloned.1.call-update) | async-done | bytes 3145744 | tf_op jit(solution)/shard_map/all_gather | solution.py:171
  702.0 11.7 multiply_convert_fusion.6
  723.1 110.4 %reduce-scatter.37.cloned.1.call-done = f32[256,1536]{1,0:T(8,128)} async-done(((f32[1024,1536]{1,0:T(8,128)}), f32[256,1536]{1,0:T(8,128)}) %reduce-scatter.37.cloned.1.call-update) | async-done | bytes 1572880 | tf_op jit(solution)/shard_map/reduce_scatter | solution.py:301
  837.6 61.0 %all-gather.39.cloned.1.call-done = bf16[1024,1536]{1,0:T(8,128)(2,1)} async-done(((bf16[256,1536]{1,0:T(8,128)(2,1)}), bf16[1024,1536]{1,0:T(8,128)(2,1)}) %all-gather.39.cloned.1.call-update) | async-done | bytes 3145744 | tf_op jit(solution)/shard_map/all_gather | solution.py:214
  898.6 8.4 fusion.120
  912.0 50.7 %all-gather.47.cloned.1.call-done = bf16[1,1024,1536]{2,1,0:T(8,128)(2,1)} async-done(((bf16[1,256,1536]{2,1,0:T(8,128)(2,1)}), bf16[1,1024,1536]{2,1,0:T(8,128)(2,1)}) %all-gather.47.cloned.1.call-update) | async-done | bytes 3145744 | tf_op jit(solution)/shard_map/all_gather | solution.py:291
  962.7 11.6 multiply_convert_fusion.4
  991.3 8.2 convolution_convert_fusion.6
  999.6 95.8 %reduce-scatter.41.cloned.1.call-done = f32[256,1536]{1,0:T(8,128)} async-done(((f32[1024,1536]{1,0:T(8,128)}), f32[256,1536]{1,0:T(8,128)}) %reduce-scatter.41.cloned.1.call-update) | async-done | bytes 1572880 | tf_op jit(solution)/shard_map/reduce_scatter | solution.py:301
  1097.7 60.1 %reduce-scatter.31.cloned.1.call-done = bf16[256,1536]{1,0:T(8,128)(2,1)} async-done(((bf16[1024,1536]{1,0:T(8,128)(2,1)}), bf16[256,1536]{1,0:T(8,128)(2,1)}) %reduce-scatter.31.cloned.1.call-update) | async-done | bytes 786448 | tf_op jit(solution)/shard_map/reduce_scatter | solution.py:218
  1157.8 63.2 %reduce-scatter.35.cloned.1.call-done = bf16[256,1536]{1,0:T(8,128)(2,1)} async-done(((bf16[1024,1536]{1,0:T(8,128)(2,1)}), bf16[256,1536]{1,0:T(8,128)(2,1)}) %reduce-scatter.35.cloned.1.call-update) | async-done | bytes 786448 | tf_op jit(solution)/shard_map/reduce_scatter | solution.py:218
  1226.8 7.8 convolution_convert_fusion.4
  1277.9 9.8 all-gather.41.cloned.1.call-done
  1291.1 60.9 %all-gather.43.cloned.1.call-done = bf16[1024,1536]{1,0:T(8,128)(2,1)} async-done(((bf16[256,1536]{1,0:T(8,128)(2,1)}), bf16[1024,1536]{1,0:T(8,128)(2,1)}) %all-gather.43.cloned.1.call-update) | async-done | bytes 3145744 | tf_op jit(solution)/shard_map/all_gather | solution.py:311
  1356.2 12.2 multiply_reduce_fusion.3
  1368.6 11.1 convert_reduce_fusion.7
  1413.8 11.6 multiply_reduce_fusion.1
  1427.9 11.5 convert_reduce_fusion.3
  1600.2 49.3 %reduce-scatter.69.cloned.1.call-done = bf16[128,1536]{1,0:T(8,128)(2,1)} async-done(((bf16[1024,1536]{1,0:T(8,128)(2,1)}), bf16[128,1536]{1,0:T(8,128)(2,1)}) %reduce-scatter.69.cloned.1.call-update) | async-done | bytes 393232 | tf_op jit(solution)/shard_map/reduce_scatter | solution.py:379
  1653.1 33.0 %reduce-scatter.75.cloned.1.call-done = bf16[192,6]{1,0:T(8,128)(2,1)} async-done(((bf16[1536,6]{1,0:T(8,128)(2,1)}), bf16[192,6]{1,0:T(8,128)(2,1)}) %reduce-scatter.75.cloned.1.call-update) | async-done | bytes 2320
  1687.0 36.2 %reduce-scatter.73.cloned.1.call-done = bf16[192,6]{1,0:T(8,128)(2,1)} async-done(((bf16[1536,6]{1,0:T(8,128)(2,1)}), bf16[192,6]{1,0:T(8,128)(2,1)}) %reduce-scatter.73.cloned.1.call-update) | async-done | bytes 2320
  1724.6 38.5 %reduce-scatter.53.cloned.1.call-done = bf16[192,384]{1,0:T(8,128)(2,1)} async-done(((bf16[1536,384]{1,0:T(8,128)(2,1)}), bf16[192,384]{1,0:T(8,128)(2,1)}) %reduce-scatter.53.cloned.1.call-update) | async-done | bytes 147472 | tf_op jit(solution)/shard_map/reduce_scatter | solution.py:364
  1763.2 39.9 %reduce-scatter.55.cloned.1.call-done = bf16[192,384]{1,0:T(8,128)(2,1)} async-done(((bf16[1536,384]{1,0:T(8,128)(2,1)}), bf16[192,384]{1,0:T(8,128)(2,1)}) %reduce-scatter.55.cloned.1.call-update) | async-done | bytes 147472 | tf_op jit(solution)/shard_map/reduce_scatter | solution.py:364
  1804.8 38.2 %reduce-scatter.51.cloned.1.call-done = bf16[192,384]{1,0:T(8,128)(2,1)} async-done(((bf16[1536,384]{1,0:T(8,128)(2,1)}), bf16[192,384]{1,0:T(8,128)(2,1)}) %reduce-scatter.51.cloned.1.call-update) | async-done | bytes 147472 | tf_op jit(solution)/shard_map/reduce_scatter | solution.py:361
  1843.1 39.8 %reduce-scatter.49.cloned.1.call-done = bf16[192,384]{1,0:T(8,128)(2,1)} async-done(((bf16[1536,384]{1,0:T(8,128)(2,1)}), bf16[192,384]{1,0:T(8,128)(2,1)}) %reduce-scatter.49.cloned.1.call-update) | async-done | bytes 147472 | tf_op jit(solution)/shard_map/reduce_scatter | solution.py:361
  1884.6 38.2 %reduce-scatter.47.cloned.1.call-done = bf16[192,384]{1,0:T(8,128)(2,1)} async-done(((bf16[1536,384]{1,0:T(8,128)(2,1)}), bf16[192,384]{1,0:T(8,128)(2,1)}) %reduce-scatter.47.cloned.1.call-update) | async-done | bytes 147472 | tf_op jit(solution)/shard_map/reduce_scatter | solution.py:358
  1922.8 39.9 %reduce-scatter.45.cloned.1.call-done = bf16[192,384]{1,0:T(8,128)(2,1)} async-done(((bf16[1536,384]{1,0:T(8,128)(2,1)}), bf16[192,384]{1,0:T(8,128)(2,1)}) %reduce-scatter.45.cloned.1.call-update) | async-done | bytes 147472 | tf_op jit(solution)/shard_map/reduce_scatter | solution.py:358
  1964.5 38.0 %reduce-scatter.59.cloned.1.call-done = bf16[48,1536]{1,0:T(8,128)(2,1)} async-done(((bf16[384,1536]{1,0:T(8,128)(2,1)}), bf16[48,1536]{1,0:T(8,128)(2,1)}) %reduce-scatter.59.cloned.1.call-update) | async-done | bytes 147472 | tf_op jit(solution)/shard_map/reduce_scatter | solution.py:370
  2002.5 39.8 %reduce-scatter.57.cloned.1.call-done = bf16[48,1536]{1,0:T(8,128)(2,1)} async-done(((bf16[384,1536]{1,0:T(8,128)(2,1)}), bf16[48,1536]{1,0:T(8,128)(2,1)}) %reduce-scatter.57.cloned.1.call-update) | async-done | bytes 147472 | tf_op jit(solution)/shard_map/reduce_scatter | solution.py:370
  2044.0 61.2 %reduce-scatter.39.cloned.1.call-done = bf16[256,1536]{1,0:T(8,128)(2,1)} async-done(((bf16[1024,1536]{1,0:T(8,128)(2,1)}), bf16[256,1536]{1,0:T(8,128)(2,1)}) %reduce-scatter.39.cloned.1.call-update) | async-done | bytes 786448 | tf_op jit(solution)/shard_map/reduce_scatter | solution.py:337
  2105.3 62.5 %reduce-scatter.43.cloned.1.call-done = bf16[256,1536]{1,0:T(8,128)(2,1)} async-done(((bf16[1024,1536]{1,0:T(8,128)(2,1)}), bf16[256,1536]{1,0:T(8,128)(2,1)}) %reduce-scatter.43.cloned.1.call-update) | async-done | bytes 786448 | tf_op jit(solution)/shard_map/reduce_scatter | solution.py:337
  2173.2 39.8 %all-reduce.2 = (f32[1536]{0:T(1024)}, f32[24]{0:T(128)}, f32[1536]{0:T(1024)}) all-reduce(f32[1536]{0:T(1024)S(1)} %add.425, f32[24]{0:T(128)S(1)} %add_dynamic-update-slice_fusion, f32[1536]{0:T(1024)S(1)} %add.432), channel_id=1, replica_groups=mesh['dp'=8,'tensor'=4] {'dp','tensor'}, use_global_device_ids=true, to_apply=%region_47.48 | all-reduce | flops 3096 | bytes 24768 | tf_op jit(solution)/shard_map/psum | solution.py:387
  (552 shorter events, 419.1 us)
Async XLA Ops:
  7.2 68.2 %all-gather.19.cloned.1.call-start = ((), (), s32[]{:S(2)}) async-start(), calls=%async_computation.24 | async-start | bytes 3932160 | tf_op jit(solution)/shard_map/all_gather | solution.py:186
  13.2 89.6 %all-gather.23.cloned.1.call-start = ((), (), s32[]{:S(2)}) async-start(), calls=%async_computation.26 | async-start | bytes 1327104 | tf_op jit(solution)/shard_map/all_gather | solution.py:164
  13.9 114.7 %all-gather.25.cloned.1.call-start = ((), (), s32[]{:S(2)}) async-start(), calls=%async_computation.27 | async-start | bytes 1327104 | tf_op jit(solution)/shard_map/all_gather | solution.py:165
  14.6 139.7 %all-gather.21.cloned.1.call-start = ((), (), s32[]{:S(2)}) async-start(), calls=%async_computation.25 | async-start | bytes 1327104 | tf_op jit(solution)/shard_map/all_gather | solution.py:166
  15.2 164.8 %all-gather.27.cloned.1.call-start = ((), (), s32[]{:S(2)}) async-start(), calls=%async_computation.28 | async-start | bytes 1327104 | tf_op jit(solution)/shard_map/all_gather | solution.py:168
  15.8 226.8 %all-gather.37.cloned.1.call-start = ((), (), s32[]{:S(2)}) async-start(), calls=%async_computation.35 | async-start | bytes 3932160 | tf_op jit(solution)/shard_map/all_gather | solution.py:186
  16.4 340.4 %reduce-scatter.29.cloned.1.call-start = ((), (), s32[]{:S(2)}) async-start(), calls=%async_computation.29 | async-start | bytes 7864320 | tf_op jit(solution)/shard_map/reduce_scatter | solution.py:206
  185.8 284.6 %reduce-scatter.33.cloned.1.call-start = ((), (), s32[]{:S(2)}) async-start(), calls=%async_computation.36 | async-start | bytes 7864320 | tf_op jit(solution)/shard_map/reduce_scatter | solution.py:206
  290.6 179.8 %copy-start.3 = (bf16[2,256,1536]{2,1,0:T(8,128)(2,1)S(1)}, bf16[2,256,1536]{2,1,0:T(8,128)(2,1)}, u32[]{:S(2)}) copy-start(bf16[2,256,1536]{2,1,0:T(8,128)(2,1)} %param.23) | copy-start | bytes 4718596
  290.6 214.9 %all-gather.33.cloned.1.call-start = ((), (), s32[]{:S(2)}) async-start(), calls=%async_computation.32 | async-start | bytes 3538944 | tf_op jit(solution)/shard_map/all_gather | solution.py:170
  291.4 182.5 %copy-start.71 = (f32[1536]{0:T(1024)S(1)}, f32[1536]{0:T(1024)}, u32[]{:S(2)}) copy-start(f32[1536]{0:T(1024)} %param.34) | copy-start | bytes 18436
  291.4 276.7 %all-gather.29.cloned.1.call-start = ((), (), s32[]{:S(2)}) async-start(), calls=%async_computation.30 | async-start | bytes 3932160 | tf_op jit(solution)/shard_map/all_gather | solution.py:214
  475.0 128.8 %all-gather.31.cloned.1.call-start = ((), (), s32[]{:S(2)}) async-start(), calls=%async_computation.31 | async-start | bytes 3538944 | tf_op jit(solution)/shard_map/all_gather | solution.py:169
  475.7 190.6 %all-gather.45.cloned.1.call-start = ((), (), s32[]{:S(2)}) async-start(), calls=%async_computation.59 | async-start | bytes 3932160 | tf_op jit(solution)/shard_map/all_gather | solution.py:291
  477.1 224.9 %all-gather.35.cloned.1.call-start = ((), (), s32[]{:S(2)}) async-start(), calls=%async_computation.33 | async-start | bytes 3538944 | tf_op jit(solution)/shard_map/all_gather | solution.py:171
  477.8 355.7 %reduce-scatter.37.cloned.1.call-start = ((), (), s32[]{:S(2)}) async-start(), calls=%async_computation.39 | async-start | bytes 7864320 | tf_op jit(solution)/shard_map/reduce_scatter | solution.py:301
  723.0 175.6 %all-gather.39.cloned.1.call-start = ((), (), s32[]{:S(2)}) async-start(), calls=%async_computation.37 | async-start | bytes 3932160 | tf_op jit(solution)/shard_map/all_gather | solution.py:214
  836.9 125.8 %all-gather.47.cloned.1.call-start = ((), (), s32[]{:S(2)}) async-start(), calls=%async_computation.60 | async-start | bytes 3932160 | tf_op jit(solution)/shard_map/all_gather | solution.py:291
  837.5 257.8 %reduce-scatter.41.cloned.1.call-start = ((), (), s32[]{:S(2)}) async-start(), calls=%async_computation.42 | async-start | bytes 7864320 | tf_op jit(solution)/shard_map/reduce_scatter | solution.py:301
  983.3 174.5 %reduce-scatter.31.cloned.1.call-start = ((), (), s32[]{:S(2)}) async-start(), calls=%async_computation.34 | async-start | bytes 3932160 | tf_op jit(solution)/shard_map/reduce_scatter | solution.py:218
  991.1 230.0 %reduce-scatter.35.cloned.1.call-start = ((), (), s32[]{:S(2)}) async-start(), calls=%async_computation.38 | async-start | bytes 3932160 | tf_op jit(solution)/shard_map/reduce_scatter | solution.py:218
  999.5 288.2 %all-gather.41.cloned.1.call-start = ((), (), s32[]{:S(2)}) async-start(), calls=%async_computation.40 | async-start | bytes 3932160 | tf_op jit(solution)/shard_map/all_gather | solution.py:311
  1226.0 125.9 %all-gather.43.cloned.1.call-start = ((), (), s32[]{:S(2)}) async-start(), calls=%async_computation.43 | async-start | bytes 3932160 | tf_op jit(solution)/shard_map/all_gather | solution.py:311
  1226.8 368.5 %reduce-scatter.63.cloned.1.call-start = ((), (), s32[]{:S(2)}) async-start(), calls=%async_computation.54 | async-start | bytes 3538944 | tf_op jit(solution)/shard_map/reduce_scatter | solution.py:373
  1234.6 360.7 %reduce-scatter.61.cloned.1.call-start = ((), (), s32[]{:S(2)}) async-start(), calls=%async_computation.53 | async-start | bytes 3538944 | tf_op jit(solution)/shard_map/reduce_scatter | solution.py:373
  1243.2 354.3 %reduce-scatter.67.cloned.1.call-start = ((), (), s32[]{:S(2)}) async-start(), calls=%async_computation.56 | async-start | bytes 3538944 | tf_op jit(solution)/shard_map/reduce_scatter | solution.py:376
  1251.6 345.9 %reduce-scatter.65.cloned.1.call-start = ((), (), s32[]{:S(2)}) async-start(), calls=%async_computation.55 | async-start | bytes 3538944 | tf_op jit(solution)/shard_map/reduce_scatter | solution.py:376
  1260.0 340.2 %reduce-scatter.71.cloned.1.call-start = ((), (), s32[]{:S(2)}) async-start(), calls=%async_computation.58 | async-start | bytes 3538944 | tf_op jit(solution)/shard_map/reduce_scatter | solution.py:379
  1268.6 380.9 %reduce-scatter.69.cloned.1.call-start = ((), (), s32[]{:S(2)}) async-start(), calls=%async_computation.57 | async-start | bytes 3538944 | tf_op jit(solution)/shard_map/reduce_scatter | solution.py:379
  1277.8 408.2 %reduce-scatter.75.cloned.1.call-start = ((), (), s32[]{:S(2)}) async-start(), calls=%async_computation.62 | async-start | bytes 442368
  1485.2 237.9 %reduce-scatter.73.cloned.1.call-start = ((), (), s32[]{:S(2)}) async-start(), calls=%async_computation.61 | async-start | bytes 442368
  1490.1 273.1 %reduce-scatter.53.cloned.1.call-start = ((), (), s32[]{:S(2)}) async-start(), calls=%async_computation.49 | async-start | bytes 1327104 | tf_op jit(solution)/shard_map/reduce_scatter | solution.py:364
  1495.1 308.0 %reduce-scatter.55.cloned.1.call-start = ((), (), s32[]{:S(2)}) async-start(), calls=%async_computation.50 | async-start | bytes 1327104 | tf_op jit(solution)/shard_map/reduce_scatter | solution.py:364
  1511.7 331.4 %reduce-scatter.51.cloned.1.call-start = ((), (), s32[]{:S(2)}) async-start(), calls=%async_computation.48 | async-start | bytes 1327104 | tf_op jit(solution)/shard_map/reduce_scatter | solution.py:361
  1524.7 358.2 %reduce-scatter.49.cloned.1.call-start = ((), (), s32[]{:S(2)}) async-start(), calls=%async_computation.47 | async-start | bytes 1327104 | tf_op jit(solution)/shard_map/reduce_scatter | solution.py:361
  1537.2 385.7 %reduce-scatter.47.cloned.1.call-start = ((), (), s32[]{:S(2)}) async-start(), calls=%async_computation.46 | async-start | bytes 1327104 | tf_op jit(solution)/shard_map/reduce_scatter | solution.py:358
  1551.7 411.0 %reduce-scatter.45.cloned.1.call-start = ((), (), s32[]{:S(2)}) async-start(), calls=%async_computation.45 | async-start | bytes 1327104 | tf_op jit(solution)/shard_map/reduce_scatter | solution.py:358
  1565.8 436.7 %reduce-scatter.59.cloned.1.call-start = ((), (), s32[]{:S(2)}) async-start(), calls=%async_computation.52 | async-start | bytes 1327104 | tf_op jit(solution)/shard_map/reduce_scatter | solution.py:370
  1570.5 471.8 %reduce-scatter.57.cloned.1.call-start = ((), (), s32[]{:S(2)}) async-start(), calls=%async_computation.51 | async-start | bytes 1327104 | tf_op jit(solution)/shard_map/reduce_scatter | solution.py:370
  1575.0 530.3 %reduce-scatter.39.cloned.1.call-start = ((), (), s32[]{:S(2)}) async-start(), calls=%async_computation.41 | async-start | bytes 3932160 | tf_op jit(solution)/shard_map/reduce_scatter | solution.py:337
  1585.1 582.7 %reduce-scatter.43.cloned.1.call-start = ((), (), s32[]{:S(2)}) async-start(), calls=%async_computation.44 | async-start | bytes 3932160 | tf_op jit(solution)/shard_map/reduce_scatter | solution.py:337
  1651.6 516.1 %copy-start.4 = (bf16[2,256,1536]{2,1,0:T(8,128)(2,1)S(1)}, bf16[2,256,1536]{2,1,0:T(8,128)(2,1)}, u32[]{:S(2)}) copy-start(bf16[2,256,1536]{2,1,0:T(8,128)(2,1)} %param.23) | copy-start | bytes 4718596
  1651.6 516.1 %copy-start.74 = (f32[1536]{0:T(1024)S(1)}, f32[1536]{0:T(1024)}, u32[]{:S(2)}) copy-start(f32[1536]{0:T(1024)} %param.27) | copy-start | bytes 18436
  1651.6 516.1 %copy-start.97 = (f32[256]{0:T(256)S(1)}, f32[256]{0:T(256)}, u32[]{:S(2)}) copy-start(f32[256]{0:T(256)} %copy-done.96) | copy-start | bytes 3076
  1651.6 516.1 %copy-start.99 = (f32[256]{0:T(256)S(1)}, f32[256]{0:T(256)}, u32[]{:S(2)}) copy-start(f32[256]{0:T(256)} %copy-done.98) | copy-start | bytes 3076
  1653.0 517.4 %copy-start.12 = (f32[256,1536]{1,0:T(8,128)S(1)}, f32[256,1536]{1,0:T(8,128)}, u32[]{:S(2)}) copy-start(f32[256,1536]{1,0:T(8,128)} %get-tuple-element.93) | copy-start | bytes 4718596
  1653.0 517.4 %copy-start.109 = (f32[256]{0:T(256)S(1)}, f32[256]{0:T(256)}, u32[]{:S(2)}) copy-start(f32[256]{0:T(256)} %get-tuple-element.145) | copy-start | bytes 3076
  1653.0 517.4 %copy-start.110 = (f32[256]{0:T(256)S(1)}, f32[256]{0:T(256)}, u32[]{:S(2)}) copy-start(f32[256]{0:T(256)} %get-tuple-element.168) | copy-start | bytes 3076
  (139 other events, 1697.3 us)
Sparse Core Ops, SparseCore 0:
  13.3 62.0 all-gather.18
  77.3 25.4 all-gather.22
  104.7 23.9 all-gather.24
  130.4 23.9 all-gather.20
  156.1 23.9 all-gather.26
  182.0 60.5 all-gather.36
  244.9 111.9 reduce-scatter.28
  359.1 111.2 reduce-scatter.32
  472.3 33.1 all-gather.32
  507.5 60.5 all-gather.28
  570.0 33.7 all-gather.30
  605.7 60.4 all-gather.44
  668.2 33.7 all-gather.34
  723.1 110.3 reduce-scatter.36
  837.1 61.4 all-gather.38
  900.6 62.0 all-gather.46
  983.4 111.8 reduce-scatter.40
  1097.5 60.2 reduce-scatter.30
  1160.7 60.2 reduce-scatter.34
  1226.2 61.5 all-gather.40
  1289.9 62.0 all-gather.42
  1355.4 47.0 reduce-scatter.62
  1405.8 46.0 reduce-scatter.60
  1455.2 46.0 reduce-scatter.66
  1504.7 46.0 reduce-scatter.64
  1554.0 46.0 reduce-scatter.70
  1603.4 46.0 reduce-scatter.68
  1652.6 33.4 reduce-scatter.74
  1689.2 33.9 reduce-scatter.72
  1726.2 36.9 reduce-scatter.52
  1766.4 36.6 reduce-scatter.54
  1806.3 36.6 reduce-scatter.50
  1846.2 36.6 reduce-scatter.48
  1886.1 36.6 reduce-scatter.46
  1926.0 36.6 reduce-scatter.44
  1965.8 36.6 reduce-scatter.58
  2005.6 36.6 reduce-scatter.56
  2045.2 60.0 reduce-scatter.38
  2107.4 60.2 reduce-scatter.42
where the time goes:
time: 2240 us; the launch traced here: 2220 us
  waiting for transfers between devices  1620 us (72%)
  matrix products  344 us (15%)
  other arithmetic  134 us (6%)
  local copies, waits for them, and re-layouts  56 us (2%)
  blocking collectives  49.5 us (2%)
    reduce_scatter x2, waiting for transfers between devices, body(): lax.psum_scatter(contract_last(grad_gate_in, full_gate) + contract_last(g...  206 us
    reduce_scatter x2, waiting for transfers between devices, body(): lax.psum_scatter(jnp.dot(mixed_flat, full_output, preferred_element_type=...  179 us
    reduce_scatter x2, waiting for transfers between devices, body(): lax.psum_scatter((total + contract_last(grad_logits, full_forget)).astype...  124 us
    all_gather x2, waiting for transfers between devices, body(): lax.all_gather(normed_two.astype(jnp.bfloat16), 'tensor', axis=0, tiled=T...  124 us
    reduce_scatter x2, waiting for transfers between devices, body(): lax.psum_scatter(jnp.dot(inner, full_down, preferred_element_type=jnp.flo...  123 us
    all_gather x2, waiting for transfers between devices, body(): upstream_all = lax.all_gather(upstream, 'tensor', axis=0, tiled=True)  105 us
    all_gather x2, waiting for transfers between devices, body(): lax.all_gather(normed.astype(jnp.bfloat16), 'tensor', axis=0, tiled=True)  98.4 us
    reduce_scatter x2, waiting for transfers between devices, body(): lax.psum_scatter(terms[2].astype(jnp.bfloat16), 'dp', scatter_dimension=0...  78.5 us
  transfers between devices with their start and end apart: 39, of which 35 were waited for; matrix products, arithmetic and copies ran while one was open for 20% of the time, Pallas kernels for 0%

commit v1 on v0

v1 whole, which is shorter than its diff:
```python
import jax
import jax.numpy as jnp
from jax import lax
from jax.sharding import PartitionSpec as P

EPS = 1e-05
NEGATIVE = -1e30
F32 = jnp.float32
BF16 = jnp.bfloat16


def rms_forward(rows, gain):
    inverse = lax.rsqrt(jnp.mean(rows * rows, axis=-1, keepdims=True) + EPS)
    return (rows * inverse * gain, inverse)


def rms_backward(rows, inverse, gain, upstream):
    scaled = upstream * gain
    return inverse * scaled - rows * inverse**3 * jnp.mean(scaled * rows, axis=-1, keepdims=True)


def dot(left, right, left_dim, right_dim):
    return lax.dot_general(
        left, right, (((left_dim,), (right_dim,)), ((), ())), preferred_element_type=F32
    )


def allowed_block(segment, present, first, size):
    length = segment.shape[0]
    places = jnp.arange(length, dtype=jnp.int32)
    query_places = first + jnp.arange(size, dtype=jnp.int32)
    query_segment = segment[first : first + size]
    allowed = (places[None, :] <= query_places[:, None]) & (
        query_segment[:, None] == segment[None, :]
    )
    return allowed & ((present[None, :] == 1) | (places[None, :] == query_places[:, None]))


def block_scores(query_block, keys_all, decay, first, size, allowed, scale):
    raw = (
        jnp.einsum("qhd,khd->hqk", query_block, keys_all, preferred_element_type=F32) * scale
    )
    raw = raw + decay[:, first : first + size, None] - decay[:, None, :]
    return jnp.where(allowed[None], raw, NEGATIVE)


def attention_forward(queries, keys_all, values_all, decay, segment, present):
    length = queries.shape[0]
    scale = queries.shape[2] ** (-0.5)
    block = min(512, length)
    mixed_blocks = []
    total_blocks = []
    for first in range(0, length, block):
        allowed = allowed_block(segment, present, first, block)
        scores = block_scores(
            queries[first : first + block], keys_all, decay, first, block, allowed, scale
        )
        highest = jnp.max(scores, axis=-1, keepdims=True)
        expo = jnp.exp(scores - highest)
        denominator = jnp.sum(expo, axis=-1, keepdims=True)
        probs = (expo / denominator).astype(BF16)
        mixed_blocks.append(
            jnp.einsum("hqk,khd->qhd", probs, values_all, preferred_element_type=F32).astype(BF16)
        )
        total_blocks.append((highest + jnp.log(denominator))[:, :, 0])
    return (jnp.concatenate(mixed_blocks, axis=0), jnp.concatenate(total_blocks, axis=1))


def attention_backward(
    queries, keys_all, values_all, decay, log_total, grad_mixed, segment, present
):
    length = queries.shape[0]
    scale = queries.shape[2] ** (-0.5)
    block = min(512, length)
    grad_keys = jnp.zeros(keys_all.shape, F32)
    grad_values = jnp.zeros(values_all.shape, F32)
    grad_decay = jnp.zeros(decay.shape, F32)
    query_grads = []
    for first in range(0, length, block):
        allowed = allowed_block(segment, present, first, block)
        query_block = queries[first : first + block]
        grad_block = grad_mixed[first : first + block]
        scores = block_scores(query_block, keys_all, decay, first, block, allowed, scale)
        probs = jnp.exp(scores - log_total[:, first : first + block, None])
        grad_values = grad_values + jnp.einsum(
            "hqk,qhd->khd", probs.astype(BF16), grad_block, preferred_element_type=F32
        )
        grad_probs = jnp.einsum("qhd,khd->hqk", grad_block, values_all, preferred_element_type=F32)
        grad_scores = probs * (grad_probs - jnp.sum(probs * grad_probs, axis=-1, keepdims=True))
        grad_low = grad_scores.astype(BF16)
        query_grads.append(
            (
                jnp.einsum("hqk,khd->qhd", grad_low, keys_all, preferred_element_type=F32) * scale
            ).astype(BF16)
        )
        grad_keys = (
            grad_keys
            + jnp.einsum("hqk,qhd->khd", grad_low, query_block, preferred_element_type=F32) * scale
        )
        as_float = grad_low.astype(F32)
        grad_decay = grad_decay.at[:, first : first + block].add(jnp.sum(as_float, axis=-1))
        grad_decay = grad_decay - jnp.sum(as_float, axis=1)
    return (
        jnp.concatenate(query_grads, axis=0),
        grad_keys.astype(BF16),
        grad_values.astype(BF16),
        grad_decay,
    )


def after(value, *others):
    return lax.optimization_barrier((value,) + others)[0]


def body(
    tokens,
    cotangent,
    segment_ids,
    slot_mask,
    attention_gain,
    query_weight,
    key_weight,
    value_weight,
    forget_weight,
    forget_bias,
    output_weight,
    swiglu_gain,
    gate_weight,
    up_weight,
    down_weight,
):
    batches, here, width = tokens.shape
    ranks = lax.axis_size("tensor")
    groups = lax.axis_size("dp")
    length = here * ranks
    heads_here = forget_weight.shape[1]
    head_width = query_weight.shape[1]
    head_size = head_width // heads_here
    units_here = gate_weight.shape[1]
    units = units_here * ranks
    unit_piece = down_weight.shape[0]
    head_piece = output_weight.shape[0]
    rank = lax.axis_index("tensor")
    bias_here = lax.dynamic_slice_in_dim(forget_bias, rank * heads_here, heads_here)

    def shift(value, step):
        if step % ranks == 0:
            return value
        return lax.ppermute(value, "tensor", [(i, (i + step) % ranks) for i in range(ranks)])

    def pieces_of(value):
        return [shift(value, step) for step in range(ranks)]

    def row_block(value, owner):
        return lax.dynamic_slice_in_dim(value, (owner % ranks) * here, here, 0)

    def place_rows(blocks, owners):
        total = jnp.zeros((length,) + blocks[0].shape[1:], blocks[0].dtype)
        for block, owner in zip(blocks, owners):
            total = lax.dynamic_update_slice_in_dim(total, block, (owner % ranks) * here, 0)
        return total

    mixed_in = jnp.concatenate((query_weight, key_weight, value_weight, forget_weight), axis=1)
    full_in = lax.all_gather(mixed_in, "dp", axis=0, tiled=True)
    output_pieces = pieces_of(output_weight)
    full_output = lax.all_gather(jnp.stack(output_pieces), "dp", axis=0)
    full_output = full_output.transpose(1, 0, 2, 3).reshape(ranks * head_width, width)
    pair = jnp.concatenate((gate_weight, up_weight), axis=1)
    pair_pieces = pieces_of(after(pair, *output_pieces))

    def by_unit(blocks):
        split = [block.reshape(block.shape[0], groups, unit_piece) for block in blocks]
        return jnp.stack(split, axis=2).reshape(blocks[0].shape[0], units)

    pair_rows = jnp.concatenate(
        (
            by_unit([piece[:, :units_here] for piece in pair_pieces]),
            by_unit([piece[:, units_here:] for piece in pair_pieces]),
        ),
        axis=1,
    )
    full_pair = lax.all_gather(pair_rows, "dp", axis=0, tiled=True)

    rows = tokens.astype(F32)
    normed, inverse_one = rms_forward(rows, attention_gain)
    normed = normed.astype(BF16)
    saved = []
    mixed_parts = []
    previous = pair_pieces
    for batch in range(batches):
        normed_pieces = pieces_of(after(normed[batch], *previous))
        previous = normed_pieces
        normed_all = place_rows(normed_pieces, [rank - step + ranks for step in range(ranks)])
        projected = dot(normed_all, full_in, 1, 0)
        queries = projected[:, :head_width].astype(BF16).reshape(length, heads_here, head_size)
        keys_all = (
            projected[:, head_width : 2 * head_width]
            .astype(BF16)
            .reshape(length, heads_here, head_size)
        )
        values_all = (
            projected[:, 2 * head_width : 3 * head_width]
            .astype(BF16)
            .reshape(length, heads_here, head_size)
        )
        logits = projected[:, 3 * head_width :] + bias_here
        decay = jnp.cumsum(jax.nn.log_sigmoid(logits), axis=0).T
        mixed, log_total = attention_forward(
            queries, keys_all, values_all, decay, segment_ids[batch], slot_mask[batch]
        )
        mixed_flat = mixed.reshape(length, head_width)
        mixed_parts.append(
            jnp.concatenate(
                [shift(row_block(mixed_flat, rank + step), step) for step in range(ranks)], axis=1
            )
        )
        saved.append((normed_all, queries, keys_all, values_all, logits, decay, log_total))
    down_pieces = pieces_of(after(down_weight, *previous))
    full_down = lax.all_gather(jnp.concatenate(down_pieces, axis=0), "dp", axis=0, tiled=True)

    mixed_here = jnp.concatenate(mixed_parts, axis=0)
    rows = rows.reshape(batches * here, width)
    upstream = cotangent.reshape(batches * here, width)
    hidden_state = rows + dot(mixed_here, full_output, 1, 0)
    normed_two, inverse_two = rms_forward(hidden_state, swiglu_gain)
    normed_two = normed_two.astype(BF16)
    both = dot(normed_two, full_pair, 1, 0)
    gate, upper = both[:, :units], both[:, units:]
    sigmoid_gate = jax.nn.sigmoid(gate)
    inner = (gate * sigmoid_gate * upper).astype(BF16)
    layer_out = (hidden_state + dot(inner, full_down, 1, 0)).astype(BF16)

    grad_inner = dot(upstream, full_down, 1, 1)
    grad_both = jnp.concatenate(
        (
            (grad_inner * upper * sigmoid_gate * (1.0 + gate * (1.0 - sigmoid_gate))).astype(BF16),
            (grad_inner * gate * sigmoid_gate).astype(BF16),
        ),
        axis=1,
    )

    def scatter(value):
        return lax.psum_scatter(value, "dp", scatter_dimension=0, tiled=True)

    def settle(blocks):
        total = blocks[0].astype(F32)
        for step in range(1, ranks):
            total = total + shift(blocks[step], ranks - step).astype(F32)
        return total

    down_rows = scatter(dot(inner, upstream, 0, 0).astype(BF16))
    pair_grad = scatter(dot(normed_two, grad_both, 0, 0).astype(BF16))
    grad_normed_two = dot(grad_both, full_pair, 1, 1)
    gain_two = jnp.sum(grad_normed_two * hidden_state * inverse_two, axis=0)
    grad_hidden = upstream.astype(F32) + rms_backward(
        hidden_state, inverse_two, swiglu_gain, grad_normed_two
    )
    branch = grad_hidden.astype(BF16)
    output_rows = dot(mixed_here, branch, 0, 0).astype(BF16)
    output_rows = output_rows.reshape(ranks, groups, head_piece, width).transpose(1, 0, 2, 3)
    output_rows = scatter(output_rows.reshape(ranks * head_width, width))
    grad_mixed_here = dot(branch, full_output, 1, 1).astype(BF16)

    projected_grads = []
    bias_grad = jnp.zeros((heads_here,), F32)
    gain_one = jnp.zeros((width,), F32)
    grad_tokens = []
    for batch in range(batches):
        normed_all, queries, keys_all, values_all, logits, decay, log_total = saved[batch]
        part = grad_mixed_here[batch * here : (batch + 1) * here]
        blocks = [
            shift(part[:, step * head_width : (step + 1) * head_width], ranks - step)
            for step in range(ranks)
        ]
        grad_mixed = place_rows(blocks, [rank + step for step in range(ranks)])
        late_queries, late_decay, grad_mixed = lax.optimization_barrier(
            (queries, decay, grad_mixed)
        )
        grad_queries, grad_keys, grad_values, grad_decay = attention_backward(
            late_queries,
            keys_all,
            values_all,
            late_decay,
            log_total,
            grad_mixed.reshape(queries.shape),
            segment_ids[batch],
            slot_mask[batch],
        )
        carried = jnp.flip(jnp.cumsum(jnp.flip(grad_decay.T, 0), axis=0), 0)
        grad_logits = (carried * jax.nn.sigmoid(-logits)).astype(BF16)
        projected_grad = jnp.concatenate(
            (
                grad_queries.reshape(length, -1),
                grad_keys.reshape(length, -1),
                grad_values.reshape(length, -1),
                grad_logits,
            ),
            axis=1,
        )
        projected_grads.append(projected_grad)
        bias_grad = bias_grad + jnp.sum(grad_logits.astype(F32), axis=0)
        partial = dot(projected_grad, full_in, 1, 1).astype(BF16)
        grad_normed = row_block(partial, rank).astype(F32)
        for step in range(1, ranks):
            grad_normed = grad_normed + shift(row_block(partial, rank + step), step).astype(F32)
        own = rows[batch * here : (batch + 1) * here]
        gain_one = gain_one + jnp.sum(grad_normed * own * inverse_one[batch], axis=0)
        grad_tokens.append(
            grad_hidden[batch * here : (batch + 1) * here]
            + rms_backward(own, inverse_one[batch], attention_gain, grad_normed)
        )
    in_grad = scatter(
        dot(
            jnp.concatenate([item[0] for item in saved], axis=0),
            jnp.concatenate(projected_grads, axis=0),
            0,
            0,
        ).astype(BF16)
    ).astype(F32)

    down_rows = down_rows.reshape(ranks, unit_piece, width)
    down_grad = settle([down_rows[step] for step in range(ranks)])
    output_rows = output_rows.reshape(ranks, head_piece, width)
    output_grad = settle([output_rows[step] for step in range(ranks)])
    split = pair_grad.reshape(pair_grad.shape[0], 2, groups, ranks, unit_piece)
    pair_grad = settle(
        [split[:, :, :, step].reshape(pair_grad.shape[0], 2 * units_here) for step in range(ranks)]
    )
    bias_full = lax.dynamic_update_slice_in_dim(
        jnp.zeros(forget_bias.shape, F32), bias_grad, rank * heads_here, 0
    )
    gain_one, gain_two, bias_full = lax.psum((gain_one, gain_two, bias_full), ("dp", "tensor"))
    return (
        layer_out.reshape(batches, here, width),
        jnp.stack(grad_tokens),
        gain_one,
        in_grad[:, :head_width],
        in_grad[:, head_width : 2 * head_width],
        in_grad[:, 2 * head_width : 3 * head_width],
        in_grad[:, 3 * head_width :],
        bias_full,
        output_grad,
        gain_two,
        pair_grad[:, :units_here],
        pair_grad[:, units_here:],
        down_grad,
    )


def solution(mesh):
    by_token = P(None, ("dp", "tensor"), None)
    by_column = P("dp", "tensor")
    by_row = P(("tensor", "dp"), None)
    weights = (by_column, by_column, by_column, by_column)
    return jax.shard_map(
        body,
        mesh=mesh,
        in_specs=(by_token, by_token, P(None, "dp"), P(None, "dp"), P())
        + weights
        + (P(), by_row, P(), by_column, by_column, by_row),
        out_specs=(by_token, by_token, P())
        + weights
        + (P(), by_row, P(), by_column, by_column, by_row),
        check_vma=False,
    )
```

time: 2240 us -> 1190 us (0.53)
  waiting for transfers between devices: 1620 us -> 530 us
  starting transfers between devices: 2.56 us -> 77.3 us
  matrix products: 344 us -> 312 us
  local copies, waits for them, and re-layouts: 56 us -> 86.6 us
  other arithmetic: 134 us -> 111 us
    reduce_scatter x22 -> x4, waiting for transfers between devices: 995 us -> 96.2 us  [scatter(): return lax.psum_scatter(value, 'dp', scatter_dimension=0, tiled=True)]
    all_gather x15 -> x4, waiting for transfers between devices: 547 us -> 0.04 us  [the longest x1 0.02 us: body(): full_pair = lax.all_gather(pair_rows, 'dp', axis=0, tiled=True)]
    ppermute x0 -> x42, waiting for transfers between devices: none -> 433 us  [shift(): lax.ppermute(value, 'tensor', [(i, (i + step) % ranks) for i in range(ran...]
    ppermute x0 -> x42, starting transfers between devices: none -> 76.4 us  [shift(): lax.ppermute(value, 'tensor', [(i, (i + step) % ranks) for i in range(ran...]
    unnamed x41 -> x8, waiting for transfers between devices: 75.9 us -> 0.13 us
    dot_general x60 -> x26, matrix products: 277 us -> 217 us  [the longest x14 164 us: dot(): lax.dot_general(left, right, (((left_dim,), (right_dim,)), ((), ())), pre...]
    dot_general x4 -> x8, matrix products: 17.4 us -> 66.8 us  [block_scores(): jnp.einsum('qhd,khd->hqk', query_block, keys_all, preferred_element_type=...]
    slice x1 -> x14, local copies, waits for them, and re-layouts: 1.24 us -> 28.2 us  [the longest x1 13.3 us: body(): split[:, :, :, step].reshape(pair_grad.shape[0], 2 * units_here)]
  transfers between devices with their start and end apart: 39 -> 50, of which waited for: 35 -> 31; matrix products, arithmetic and copies ran while one was open for 20% -> 28% of each run, Pallas kernels for 0% -> 0%
where the time goes in v1:
time: 1190 us; the launch traced here: 1180 us
  waiting for transfers between devices  530 us (45%)
  matrix products  312 us (26%)
  other arithmetic  111 us (9%)
  local copies, waits for them, and re-layouts  86.6 us (7%)
  starting transfers between devices  77.3 us (6%)
  blocking collectives  43 us (4%)
  between operations  16.2 us (1%)
    ppermute x42, waiting for transfers between devices, shift(): lax.ppermute(value, 'tensor', [(i, (i + step) % ranks) for i in range(ran...  433 us
    dot_general x14, matrix products, dot(): lax.dot_general(left, right, (((left_dim,), (right_dim,)), ((), ())), pre...  164 us
    reduce_scatter x4, waiting for transfers between devices, scatter(): return lax.psum_scatter(value, 'dp', scatter_dimension=0, tiled=True)  96.2 us
    ppermute x42, starting transfers between devices, shift(): lax.ppermute(value, 'tensor', [(i, (i + step) % ranks) for i in range(ran...  76.4 us
    dot_general x8, matrix products, block_scores(): jnp.einsum('qhd,khd->hqk', query_block, keys_all, preferred_element_type=...  66.8 us
    psum x1, blocking collectives, body(): lax.psum((gain_one, gain_two, bias_full), ('dp', 'tensor'))  43 us
    dot_general x4, matrix products, attention_forward(): jnp.einsum('hqk,khd->qhd', probs, values_all, preferred_element_type=F32)  25.8 us
  transfers between devices with their start and end apart: 50, of which 31 were waited for; matrix products, arithmetic and copies ran while one was open for 28% of the time, Pallas kernels for 0%

profile of v1, /device:TPU:9, one launch (start us, length us, event | category | flops | bytes accessed | tf_op | source)
XLA Modules:
  0.0 1175.1 jit_solution(16808823180732013417)
XLA Ops:
  15.0 6.9 collective-permute-done.1
  33.8 13.7 %collective-permute-done.5 = bf16[192,2048]{1,0:T(8,128)(2,1)} collective-permute-done((bf16[192,2048]{1,0:T(8,128)(2,1)S(1)}, bf16[192,2048]{1,0:T(8,128)(2,1)}, u32[]{:S(2)}, u32[]{:S(2)}) %collective-permute-start.5) | collective-permute-done | bytes 786464 | tf_op jit(solution)/shard_map/ppermute | solution.py:149
  50.6 29.5 %collective-permute-done.4 = bf16[192,2048]{1,0:T(8,128)(2,1)} collective-permute-done((bf16[192,2048]{1,0:T(8,128)(2,1)S(1)}, bf16[192,2048]{1,0:T(8,128)(2,1)}, u32[]{:S(2)}, u32[]{:S(2)}) %collective-permute-start.4) | collective-permute-done | bytes 786464 | tf_op jit(solution)/shard_map/ppermute | solution.py:149
  84.5 12.5 %collective-permute-done.3 = bf16[192,2048]{1,0:T(8,128)(2,1)} collective-permute-done((bf16[192,2048]{1,0:T(8,128)(2,1)S(1)}, bf16[192,2048]{1,0:T(8,128)(2,1)}, u32[]{:S(2)}, u32[]{:S(2)}) %collective-permute-start.3) | collective-permute-done | bytes 786464 | tf_op jit(solution)/shard_map/ppermute | solution.py:149
  125.0 6.7 collective-permute-start.8
  139.6 7.7 collective-permute-done.8
  147.3 35.2 %collective-permute-done.7 = bf16[256,1536]{1,0:T(8,128)(2,1)S(1)} collective-permute-done((bf16[256,1536]{1,0:T(8,128)(2,1)S(1)}, bf16[256,1536]{1,0:T(8,128)(2,1)S(1)}, u32[]{:S(2)}, u32[]{:S(2)}) %collective-permute-start.7) | collective-permute-done | bytes 786464 | tf_op jit(solution)/shard_map/ppermute | solution.py:149
  182.4 33.7 %collective-permute-done.6 = bf16[256,1536]{1,0:T(8,128)(2,1)S(1)} collective-permute-done((bf16[256,1536]{1,0:T(8,128)(2,1)S(1)}, bf16[256,1536]{1,0:T(8,128)(2,1)S(1)}, u32[]{:S(2)}, u32[]{:S(2)}) %collective-permute-start.6) | collective-permute-done | bytes 786464 | tf_op jit(solution)/shard_map/ppermute | solution.py:149
  225.3 10.8 collective-permute-done.14
  236.1 17.7 %collective-permute-done.13 = bf16[256,1536]{1,0:T(8,128)(2,1)S(1)} collective-permute-done((bf16[256,1536]{1,0:T(8,128)(2,1)S(1)}, bf16[256,1536]{1,0:T(8,128)(2,1)S(1)}, u32[]{:S(2)}, u32[]{:S(2)}) %collective-permute-start.13) | collective-permute-done | bytes 786464 | tf_op jit(solution)/shard_map/ppermute | solution.py:149
  253.8 16.5 %collective-permute-done.12 = bf16[256,1536]{1,0:T(8,128)(2,1)S(1)} collective-permute-done((bf16[256,1536]{1,0:T(8,128)(2,1)S(1)}, bf16[256,1536]{1,0:T(8,128)(2,1)S(1)}, u32[]{:S(2)}, u32[]{:S(2)}) %collective-permute-start.12) | collective-permute-done | bytes 786464 | tf_op jit(solution)/shard_map/ppermute | solution.py:149
  270.3 17.4 %collective-permute-start.20 = (bf16[128,1536]{1,0:T(8,128)(2,1)S(1)}, bf16[128,1536]{1,0:T(8,128)(2,1)S(1)}, u32[]{:S(2)}, u32[]{:S(2)}) collective-permute-start(bf16[128,1536]{1,0:T(8,128)(2,1)S(1)} %copy-done.58), channel_id=1, source_target_pairs={{0,3},{1,0},{2,1},{3,2},{4,7},{5,4},{6,5},{7,6},{8,11},{9,8},{10,9... | collective-permute-start | bytes 1179656 | tf_op jit(solution)/shard_map/ppermute | solution.py:149
  295.8 17.4 %collective-permute-done.19 = bf16[128,1536]{1,0:T(8,128)(2,1)S(1)} collective-permute-done((bf16[128,1536]{1,0:T(8,128)(2,1)S(1)}, bf16[128,1536]{1,0:T(8,128)(2,1)S(1)}, u32[]{:S(2)}, u32[]{:S(2)}) %collective-permute-start.19) | collective-permute-done | bytes 393248 | tf_op jit(solution)/shard_map/ppermute | solution.py:149
  313.2 8.4 collective-permute-done.18
  323.0 8.8 fusion.150
  331.7 9.5 fusion.151
  358.6 11.5 fusion
  374.7 8.0 fusion.92
  393.5 6.6 fusion.11
  400.1 10.5 fusion.2
  415.3 8.0 fusion.94
  453.7 22.6 %fusion.127 = f32[512,8192]{1,0:T(8,128)} fusion(bf16[1536,8192]{1,0:T(8,128)(2,1)} %all-gather.8.cloned.1.call-done, f32[512,1536]{1,0:T(8,128)} %get-tuple-element.271, f32[1536]{0:T(1024)S(1)} %copy-done.71, f32[512]{0:T(512)S(1)} %get-tuple-element.253), kind=kOutput, calls=%fused_computation.302 | convolution fusion | flops 12887261184 | bytes 45096960 | tf_op jit(solution)/shard_map/dot_general | solution.py:23
  476.3 19.3 %fusion.6 = (bf16[512,4096]{1,0:T(8,128)(2,1)}, bf16[512,4096]{1,0:T(8,128)(2,1)}, bf16[512,4096]{1,0:T(8,128)(2,1)}) fusion(f32[512,8192]{1,0:T(8,128)} %fusion.127, bf16[4096,1536]{1,0:T(8,128)(2,1)} %all-gather.10.cloned.1.call-done, bf16[512,1536]{1,0:T(8,128)(2,1)} %bitcast.292), kind=kOutput, calls=%fused_computation.43 | convolution fusion | flops 6476005376 | bytes 43515904 | tf_op jit(solution)/shard_map/dot_general | solution.py:23
  495.6 21.5 %multiply_reduce_fusion.4 = (f32[1536]{0:T(1024)}, f32[512]{0:T(512)S(1)}, f32[512,1536]{1,0:T(8,128)}) fusion(f32[512,1536]{1,0:T(8,128)S(1)} %copy-done.35, f32[512]{0:T(512)S(1)} %get-tuple-element.253, f32[1536]{0:T(1024)S(1)} %copy-done.71, bf16[1536,8192]{1,0:T(8,128)(2,1)} %all-gather.8.cloned.1.call-done, bf16[512,4096]{1,0:T(8,128)(2,1)} %get-tuple-element.172, ...), kind=kOutput, calls=%fused_computation.91 | convolution fusion | flops 12906395648 | bytes 39862272 | tf_op jit(solution)/shard_map/dot_general | solution.py:23
  529.7 20.1 %collective-permute-done.21 = bf16[256,384]{1,0:T(8,128)(2,1)S(1)} collective-permute-done((bf16[256,384]{1,0:T(8,128)(2,1)S(1)}, bf16[256,384]{1,0:T(8,128)(2,1)S(1)}, u32[]{:S(2)}, u32[]{:S(2)}) %collective-permute-start.21) | collective-permute-done | bytes 196640 | tf_op jit(solution)/shard_map/ppermute | solution.py:149
  549.9 7.2 collective-permute-done.23
  565.2 8.7 multiply_reduce_fusion.3
  573.9 10.4 convert_reduce_fusion.7
  596.8 7.7 multiply_reduce_fusion.1
  604.5 10.6 convert_reduce_fusion.3
  623.6 7.7 multiply_reduce_fusion.2
  642.0 6.9 add_convert_fusion.1
  659.7 7.7 multiply_reduce_fusion
  677.3 6.8 add_convert_fusion
  696.6 14.2 %convolution_convert_fusion.3 = bf16[1536,1158]{1,0:T(8,128)(2,1)} fusion(bf16[1024,1536]{1,0:T(8,128)(2,1)} %constant_dynamic-update-slice_fusion.6, bf16[1024,1536]{1,0:T(8,128)(2,1)} %constant_dynamic-update-slice_fusion.10, bf16[1024,6]{0,1:T(8,128)(2,1)} %get-tuple-element.162, bf16[1024,384]{0,1:T(8,128)(2,1)} %bitcast.303, ...), kind=kOutput, calls=%fused_computation.49 | convolution fusion | flops 7337812992 | bytes 14592000 | tf_op jit(solution)/shard_map/dot_general | solution.py:23
  719.3 12.3 %convolution_convert_fusion.1 = bf16[4096,1536]{1,0:T(8,128)(2,1)} fusion(bf16[512,4096]{1,0:T(8,128)(2,1)} %get-tuple-element.173, bf16[512,1536]{1,0:T(8,128)(2,1)S(1)} %bitcast.293), kind=kOutput, calls=%fused_computation.9 | convolution fusion | flops 6448742400 | bytes 18350080 | tf_op jit(solution)/shard_map/dot_general | solution.py:23
  733.5 21.4 %convolution_convert_fusion = bf16[1536,8192]{1,0:T(8,128)(2,1)} fusion(bf16[512,4096]{1,0:T(8,128)(2,1)} %get-tuple-element.172, bf16[512,4096]{1,0:T(8,128)(2,1)} %get-tuple-element.171, f32[512,1536]{1,0:T(8,128)S(1)} %copy-done.36, f32[1536]{0:T(1024)S(1)} %copy-done.72, f32[512]{0:T(512)S(1)} %copy-done.74), kind=kOutput, calls=%fused_computation | convolution fusion | flops 12916621312 | bytes 36708352 | tf_op jit(solution)/shard_map/dot_general | solution.py:23
  756.5 6.9 convolution_convert_fusion.4
  774.6 7.9 collective-permute-done.30
  786.8 10.8 fusion.44
  802.1 31.0 %collective-permute-done.31 = bf16[256,1536]{1,0:T(8,128)(2,1)S(1)} collective-permute-done((bf16[256,1536]{1,0:T(8,128)(2,1)S(1)}, bf16[256,1536]{1,0:T(8,128)(2,1)S(1)}, u32[]{:S(2)}, u32[]{:S(2)}) %collective-permute-start.31) | collective-permute-done | bytes 786464 | tf_op jit(solution)/shard_map/ppermute | solution.py:149
  833.1 49.8 %collective-permute-done.24 = bf16[256,1536]{1,0:T(8,128)(2,1)S(1)} collective-permute-done((bf16[256,1536]{1,0:T(8,128)(2,1)S(1)}, bf16[256,1536]{1,0:T(8,128)(2,1)S(1)}, u32[]{:S(2)}, u32[]{:S(2)}) %collective-permute-start.24) | collective-permute-done | bytes 786464 | tf_op jit(solution)/shard_map/ppermute | solution.py:149
  885.7 14.0 %collective-permute-done.25 = bf16[256,1536]{1,0:T(8,128)(2,1)S(1)} collective-permute-done((bf16[256,1536]{1,0:T(8,128)(2,1)S(1)}, bf16[256,1536]{1,0:T(8,128)(2,1)S(1)}, u32[]{:S(2)}, u32[]{:S(2)}) %collective-permute-start.25) | collective-permute-done | bytes 786464 | tf_op jit(solution)/shard_map/ppermute | solution.py:149
  902.7 43.0 %all-reduce.2 = (f32[1536]{0:T(1024)}, f32[24]{0:T(128)}, f32[1536]{0:T(1024)}) all-reduce(f32[1536]{0:T(1024)S(1)} %add.500, f32[24]{0:T(128)S(1)} %add_dynamic-update-slice_fusion, f32[1536]{0:T(1024)S(1)} %copy-done.76), channel_id=1, replica_groups=mesh['dp'=8,'tensor'=4] {'dp','tensor'}, use_global_device_ids=true, to_apply=%region_36.37 | all-reduce | flops 3096 | bytes 24768 | tf_op jit(solution)/shard_map/psum | solution.py:332
  979.7 96.2 %reduce-scatter.9.cloned.1.call-done = bf16[192,8192]{1,0:T(8,128)(2,1)} async-done(((bf16[1536,8192]{1,0:T(8,128)(2,1)}), bf16[192,8192]{1,0:T(8,128)(2,1)}) %reduce-scatter.9.cloned.1.call-update) | async-done | bytes 3145744 | tf_op jit(solution)/shard_map/reduce_scatter | solution.py:243
  1080.6 13.3 %slice_reduce_fusion.2 = (bf16[192,2,8,128]{3,2,1,0:T(8,128)(2,1)S(1)}, bf16[192,2,8,128]{3,2,1,0:T(8,128)(2,1)S(1)}, bf16[192,2,8,128]{3,2,1,0:T(8,128)(2,1)S(1)}) fusion(bf16[192,2,8,4,128]{4,3,2,1,0:T(4,128)(2,1)S(1)} %reshape.777), kind=kLoop, calls=%fused_computation.135 | loop fusion | bytes 4718592 | tf_op jit(solution)/shard_map/slice | solution.py:327
  1104.9 7.9 collective-permute-done.38
  1112.9 49.5 %collective-permute-done.37 = bf16[192,2048]{1,0:T(8,128)(2,1)S(1)} collective-permute-done((bf16[192,2048]{1,0:T(8,128)(2,1)S(1)}, bf16[192,2048]{1,0:T(8,128)(2,1)S(1)}, u32[]{:S(2)}, u32[]{:S(2)}) %collective-permute-start.37) | collective-permute-done | bytes 786464 | tf_op jit(solution)/shard_map/ppermute | solution.py:149
  (434 shorter events, 326.7 us)
Async XLA Ops:
  7.2 315.8 %all-gather.6.cloned.1.call-start = ((), (), s32[]{:S(2)}) async-start(), calls=%async_computation.4 | async-start | bytes 4423680 | tf_op jit(solution)/shard_map/all_gather | solution.py:164
  10.0 425.6 %all-gather.12.cloned.1.call-start = ((), (), s32[]{:S(2)}) async-start(), calls=%async_computation.11 | async-start | bytes 5308416 | tf_op jit(solution)/shard_map/all_gather | solution.py:166
  10.1 11.8 %collective-permute-start.1 = (bf16[48,1536]{1,0:T(8,128)(2,1)}, bf16[48,1536]{1,0:T(8,128)(2,1)S(1)}, u32[]{:S(2)}, u32[]{:S(2)}) collective-permute-start(bf16[48,1536]{1,0:T(8,128)(2,1)} %param.33), channel_id=1, source_target_pairs={{0,2},{1,3},{2,0},{3,1},{4,6},{5,7},{6,4},{7,5},{8,10},{9,11},{10,... | collective-permute-start | bytes 442376 | tf_op jit(solution)/shard_map/ppermute | solution.py:149
  12.6 12.7 %collective-permute-start = (bf16[48,1536]{1,0:T(8,128)(2,1)}, bf16[48,1536]{1,0:T(8,128)(2,1)S(1)}, u32[]{:S(2)}, u32[]{:S(2)}) collective-permute-start(bf16[48,1536]{1,0:T(8,128)(2,1)} %param.33), channel_id=1, source_target_pairs={{0,1},{1,2},{2,3},{3,0},{4,5},{5,6},{6,7},{7,4},{8,9},{9,10},{10,1... | collective-permute-start | bytes 442376 | tf_op jit(solution)/shard_map/ppermute | solution.py:149
  27.1 426.6 %all-gather.8.cloned.1.call-start = ((), (), s32[]{:S(2)}) async-start(), calls=%async_computation.5 | async-start | bytes 28311552 | tf_op jit(solution)/shard_map/all_gather | solution.py:182
  28.3 19.2 %collective-permute-start.5 = (bf16[192,2048]{1,0:T(8,128)(2,1)S(1)}, bf16[192,2048]{1,0:T(8,128)(2,1)}, u32[]{:S(2)}, u32[]{:S(2)}) collective-permute-start(bf16[192,2048]{1,0:T(8,128)(2,1)S(1)} %pad_maximum_fusion.8), channel_id=1, source_target_pairs={{0,3},{1,0},{2,1},{3,2},{4,7},{5,4},{6,5},{7,6},{8,11},{9,8},{10,9... | collective-permute-start | bytes 2359304 | tf_op jit(solution)/shard_map/ppermute | solution.py:149
  29.3 50.8 %collective-permute-start.4 = (bf16[192,2048]{1,0:T(8,128)(2,1)S(1)}, bf16[192,2048]{1,0:T(8,128)(2,1)}, u32[]{:S(2)}, u32[]{:S(2)}) collective-permute-start(bf16[192,2048]{1,0:T(8,128)(2,1)S(1)} %pad_maximum_fusion.8), channel_id=1, source_target_pairs={{0,2},{1,3},{2,0},{3,1},{4,6},{5,7},{6,4},{7,5},{8,10},{9,11},{10,... | collective-permute-start | bytes 2359304 | tf_op jit(solution)/shard_map/ppermute | solution.py:149
  31.7 65.2 %collective-permute-start.3 = (bf16[192,2048]{1,0:T(8,128)(2,1)S(1)}, bf16[192,2048]{1,0:T(8,128)(2,1)}, u32[]{:S(2)}, u32[]{:S(2)}) collective-permute-start(bf16[192,2048]{1,0:T(8,128)(2,1)S(1)} %pad_maximum_fusion.8), channel_id=1, source_target_pairs={{0,1},{1,2},{2,3},{3,0},{4,5},{5,6},{6,7},{7,4},{8,9},{9,10},{10,1... | collective-permute-start | bytes 2359304 | tf_op jit(solution)/shard_map/ppermute | solution.py:149
  118.2 358.2 %all-gather.10.cloned.1.call-start = ((), (), s32[]{:S(2)}) async-start(), calls=%async_computation.6 | async-start | bytes 14155776 | tf_op jit(solution)/shard_map/all_gather | solution.py:219
  125.0 22.3 %collective-permute-start.8 = (bf16[256,1536]{1,0:T(8,128)(2,1)S(1)}, bf16[256,1536]{1,0:T(8,128)(2,1)S(1)}, u32[]{:S(2)}, u32[]{:S(2)}) collective-permute-start(bf16[256,1536]{1,0:T(8,128)(2,1)S(1)} %get-tuple-element.72), channel_id=1, source_target_pairs={{0,3},{1,0},{2,1},{3,2},{4,7},{5,4},{6,5},{7,6},{8,11},{9,8},{10,9... | collective-permute-start | bytes 2359304 | tf_op jit(solution)/shard_map/ppermute | solution.py:149
  131.7 50.7 %collective-permute-start.7 = (bf16[256,1536]{1,0:T(8,128)(2,1)S(1)}, bf16[256,1536]{1,0:T(8,128)(2,1)S(1)}, u32[]{:S(2)}, u32[]{:S(2)}) collective-permute-start(bf16[256,1536]{1,0:T(8,128)(2,1)S(1)} %get-tuple-element.72), channel_id=1, source_target_pairs={{0,2},{1,3},{2,0},{3,1},{4,6},{5,7},{6,4},{7,5},{8,10},{9,11},{10,... | collective-permute-start | bytes 2359304 | tf_op jit(solution)/shard_map/ppermute | solution.py:149
  131.7 84.4 %collective-permute-start.6 = (bf16[256,1536]{1,0:T(8,128)(2,1)S(1)}, bf16[256,1536]{1,0:T(8,128)(2,1)S(1)}, u32[]{:S(2)}, u32[]{:S(2)}) collective-permute-start(bf16[256,1536]{1,0:T(8,128)(2,1)S(1)} %get-tuple-element.72), channel_id=1, source_target_pairs={{0,1},{1,2},{2,3},{3,0},{4,5},{5,6},{6,7},{7,4},{8,9},{9,10},{10,1... | collective-permute-start | bytes 2359304 | tf_op jit(solution)/shard_map/ppermute | solution.py:149
  216.2 19.9 %collective-permute-start.14 = (bf16[256,1536]{1,0:T(8,128)(2,1)S(1)}, bf16[256,1536]{1,0:T(8,128)(2,1)S(1)}, u32[]{:S(2)}, u32[]{:S(2)}) collective-permute-start(bf16[256,1536]{1,0:T(8,128)(2,1)S(1)} %get-tuple-element.73), channel_id=1, source_target_pairs={{0,3},{1,0},{2,1},{3,2},{4,7},{5,4},{6,5},{7,6},{8,11},{9,8},{10,9... | collective-permute-start | bytes 2359304 | tf_op jit(solution)/shard_map/ppermute | solution.py:149
  216.2 37.6 %collective-permute-start.13 = (bf16[256,1536]{1,0:T(8,128)(2,1)S(1)}, bf16[256,1536]{1,0:T(8,128)(2,1)S(1)}, u32[]{:S(2)}, u32[]{:S(2)}) collective-permute-start(bf16[256,1536]{1,0:T(8,128)(2,1)S(1)} %get-tuple-element.73), channel_id=1, source_target_pairs={{0,2},{1,3},{2,0},{3,1},{4,6},{5,7},{6,4},{7,5},{8,10},{9,11},{10,... | collective-permute-start | bytes 2359304 | tf_op jit(solution)/shard_map/ppermute | solution.py:149
  219.6 50.7 %collective-permute-start.12 = (bf16[256,1536]{1,0:T(8,128)(2,1)S(1)}, bf16[256,1536]{1,0:T(8,128)(2,1)S(1)}, u32[]{:S(2)}, u32[]{:S(2)}) collective-permute-start(bf16[256,1536]{1,0:T(8,128)(2,1)S(1)} %get-tuple-element.73), channel_id=1, source_target_pairs={{0,1},{1,2},{2,3},{3,0},{4,5},{5,6},{6,7},{7,4},{8,9},{9,10},{10,1... | collective-permute-start | bytes 2359304 | tf_op jit(solution)/shard_map/ppermute | solution.py:149
  270.3 25.5 %collective-permute-start.20 = (bf16[128,1536]{1,0:T(8,128)(2,1)S(1)}, bf16[128,1536]{1,0:T(8,128)(2,1)S(1)}, u32[]{:S(2)}, u32[]{:S(2)}) collective-permute-start(bf16[128,1536]{1,0:T(8,128)(2,1)S(1)} %copy-done.58), channel_id=1, source_target_pairs={{0,3},{1,0},{2,1},{3,2},{4,7},{5,4},{6,5},{7,6},{8,11},{9,8},{10,9... | collective-permute-start | bytes 1179656 | tf_op jit(solution)/shard_map/ppermute | solution.py:149
  287.7 25.5 %collective-permute-start.19 = (bf16[128,1536]{1,0:T(8,128)(2,1)S(1)}, bf16[128,1536]{1,0:T(8,128)(2,1)S(1)}, u32[]{:S(2)}, u32[]{:S(2)}) collective-permute-start(bf16[128,1536]{1,0:T(8,128)(2,1)S(1)} %copy-done.58), channel_id=1, source_target_pairs={{0,2},{1,3},{2,0},{3,1},{4,6},{5,7},{6,4},{7,5},{8,10},{9,11},{10,... | collective-permute-start | bytes 1179656 | tf_op jit(solution)/shard_map/ppermute | solution.py:149
  287.7 33.9 %collective-permute-start.18 = (bf16[128,1536]{1,0:T(8,128)(2,1)S(1)}, bf16[128,1536]{1,0:T(8,128)(2,1)S(1)}, u32[]{:S(2)}, u32[]{:S(2)}) collective-permute-start(bf16[128,1536]{1,0:T(8,128)(2,1)S(1)} %copy-done.58), channel_id=1, source_target_pairs={{0,1},{1,2},{2,3},{3,0},{4,5},{5,6},{6,7},{7,4},{8,9},{9,10},{10,1... | collective-permute-start | bytes 1179656 | tf_op jit(solution)/shard_map/ppermute | solution.py:149
  322.9 629.9 %reduce-scatter.5.cloned.1.call-start = ((), (), s32[]{:S(2)}) async-start(), calls=%async_computation.7 | async-start | bytes 4423680 | tf_op jit(solution)/shard_map/reduce_scatter | solution.py:243
  388.6 43.3 %collective-permute-start.11 = (bf16[256,384]{0,1:T(8,128)(2,1)S(1)}, bf16[256,384]{0,1:T(8,128)(2,1)S(1)}, u32[]{:S(2)}, u32[]{:S(2)}) collective-permute-start(bf16[256,384]{0,1:T(8,128)(2,1)S(1)} %get-tuple-element.219), channel_id=1, source_target_pairs={{0,3},{1,0},{2,1},{3,2},{4,7},{5,4},{6,5},{7,6},{8,11},{9,8},{10,9... | collective-permute-start | bytes 589832 | tf_op jit(solution)/shard_map/ppermute | solution.py:149
  388.6 49.7 %collective-permute-start.10 = (bf16[256,384]{0,1:T(8,128)(2,1)}, bf16[256,384]{0,1:T(8,128)(2,1)}, u32[]{:S(2)}, u32[]{:S(2)}) collective-permute-start(bf16[256,384]{0,1:T(8,128)(2,1)} %get-tuple-element.220), channel_id=1, source_target_pairs={{0,2},{1,3},{2,0},{3,1},{4,6},{5,7},{6,4},{7,5},{8,10},{9,11},{10,... | collective-permute-start | bytes 589832 | tf_op jit(solution)/shard_map/ppermute | solution.py:149
  392.3 46.0 %collective-permute-start.9 = (bf16[256,384]{0,1:T(8,128)(2,1)}, bf16[256,384]{0,1:T(8,128)(2,1)}, u32[]{:S(2)}, u32[]{:S(2)}) collective-permute-start(bf16[256,384]{0,1:T(8,128)(2,1)} %get-tuple-element.221), channel_id=1, source_target_pairs={{0,1},{1,2},{2,3},{3,0},{4,5},{5,6},{6,7},{7,4},{8,9},{9,10},{10,1... | collective-permute-start | bytes 589832 | tf_op jit(solution)/shard_map/ppermute | solution.py:149
  429.2 9.1 collective-permute-start.17
  430.7 13.1 %collective-permute-start.16 = (bf16[256,384]{0,1:T(8,128)(2,1)}, bf16[256,384]{0,1:T(8,128)(2,1)}, u32[]{:S(2)}, u32[]{:S(2)}) collective-permute-start(bf16[256,384]{0,1:T(8,128)(2,1)} %get-tuple-element.224), channel_id=1, source_target_pairs={{0,2},{1,3},{2,0},{3,1},{4,6},{5,7},{6,4},{7,5},{8,10},{9,11},{10,... | collective-permute-start | bytes 589832 | tf_op jit(solution)/shard_map/ppermute | solution.py:149
  432.6 15.4 %collective-permute-start.15 = (bf16[256,384]{0,1:T(8,128)(2,1)}, bf16[256,384]{0,1:T(8,128)(2,1)}, u32[]{:S(2)}, u32[]{:S(2)}) collective-permute-start(bf16[256,384]{0,1:T(8,128)(2,1)} %get-tuple-element.225), channel_id=1, source_target_pairs={{0,1},{1,2},{2,3},{3,0},{4,5},{5,6},{6,7},{7,4},{8,9},{9,10},{10,1... | collective-permute-start | bytes 589832 | tf_op jit(solution)/shard_map/ppermute | solution.py:149
  523.8 26.0 %collective-permute-start.22 = (bf16[256,384]{1,0:T(8,128)(2,1)S(1)}, bf16[256,384]{1,0:T(8,128)(2,1)S(1)}, u32[]{:S(2)}, u32[]{:S(2)}) collective-permute-start(bf16[256,384]{1,0:T(8,128)(2,1)S(1)} %get-tuple-element.202), channel_id=1, source_target_pairs={{0,2},{1,3},{2,0},{3,1},{4,6},{5,7},{6,4},{7,5},{8,10},{9,11},{10,... | collective-permute-start | bytes 589832 | tf_op jit(solution)/shard_map/ppermute | solution.py:149
  523.9 25.9 %collective-permute-start.21 = (bf16[256,384]{1,0:T(8,128)(2,1)S(1)}, bf16[256,384]{1,0:T(8,128)(2,1)S(1)}, u32[]{:S(2)}, u32[]{:S(2)}) collective-permute-start(bf16[256,384]{1,0:T(8,128)(2,1)S(1)} %get-tuple-element.203), channel_id=1, source_target_pairs={{0,3},{1,0},{2,1},{3,2},{4,7},{5,4},{6,5},{7,6},{8,11},{9,8},{10,9... | collective-permute-start | bytes 589832 | tf_op jit(solution)/shard_map/ppermute | solution.py:149
  527.4 64.3 %collective-permute-start.29 = (bf16[256,384]{1,0:T(8,128)(2,1)S(1)}, bf16[256,384]{1,0:T(8,128)(2,1)}, u32[]{:S(2)}, u32[]{:S(2)}) collective-permute-start(bf16[256,384]{1,0:T(8,128)(2,1)S(1)} %get-tuple-element.197), channel_id=1, source_target_pairs={{0,1},{1,2},{2,3},{3,0},{4,5},{5,6},{6,7},{7,4},{8,9},{9,10},{10,1... | collective-permute-start | bytes 589832 | tf_op jit(solution)/shard_map/ppermute | solution.py:149
  527.5 63.0 %collective-permute-start.28 = (bf16[256,384]{1,0:T(8,128)(2,1)S(1)}, bf16[256,384]{1,0:T(8,128)(2,1)}, u32[]{:S(2)}, u32[]{:S(2)}) collective-permute-start(bf16[256,384]{1,0:T(8,128)(2,1)S(1)} %get-tuple-element.198), channel_id=1, source_target_pairs={{0,2},{1,3},{2,0},{3,1},{4,6},{5,7},{6,4},{7,5},{8,10},{9,11},{10,... | collective-permute-start | bytes 589832 | tf_op jit(solution)/shard_map/ppermute | solution.py:149
  529.7 59.8 %collective-permute-start.27 = (bf16[256,384]{1,0:T(8,128)(2,1)S(1)}, bf16[256,384]{1,0:T(8,128)(2,1)}, u32[]{:S(2)}, u32[]{:S(2)}) collective-permute-start(bf16[256,384]{1,0:T(8,128)(2,1)S(1)} %get-tuple-element.199), channel_id=1, source_target_pairs={{0,3},{1,0},{2,1},{3,2},{4,7},{5,4},{6,5},{7,6},{8,11},{9,8},{10,9... | collective-permute-start | bytes 589832 | tf_op jit(solution)/shard_map/ppermute | solution.py:149
  549.8 7.3 collective-permute-start.23
  710.8 243.5 %reduce-scatter.7.cloned.1.call-start = ((), (), s32[]{:S(2)}) async-start(), calls=%async_computation.8 | async-start | bytes 5308416 | tf_op jit(solution)/shard_map/reduce_scatter | solution.py:243
  717.7 253.1 %reduce-scatter.11.cloned.1.call-start = ((), (), s32[]{:S(2)}) async-start(), calls=%async_computation.10 | async-start | bytes 14155776 | tf_op jit(solution)/shard_map/reduce_scatter | solution.py:243
  731.6 344.3 %reduce-scatter.9.cloned.1.call-start = ((), (), s32[]{:S(2)}) async-start(), calls=%async_computation.9 | async-start | bytes 28311552 | tf_op jit(solution)/shard_map/reduce_scatter | solution.py:243
  763.6 19.0 %collective-permute-start.30 = (bf16[256,1536]{1,0:T(8,128)(2,1)S(1)}, bf16[256,1536]{1,0:T(8,128)(2,1)S(1)}, u32[]{:S(2)}, u32[]{:S(2)}) collective-permute-start(bf16[256,1536]{1,0:T(8,128)(2,1)S(1)} %get-tuple-element.176), channel_id=1, source_target_pairs={{0,1},{1,2},{2,3},{3,0},{4,5},{5,6},{6,7},{7,4},{8,9},{9,10},{10,1... | collective-permute-start | bytes 2359304 | tf_op jit(solution)/shard_map/ppermute | solution.py:149
  765.8 36.3 %collective-permute-start.32 = (bf16[256,1536]{1,0:T(8,128)(2,1)S(1)}, bf16[256,1536]{1,0:T(8,128)(2,1)S(1)}, u32[]{:S(2)}, u32[]{:S(2)}) collective-permute-start(bf16[256,1536]{1,0:T(8,128)(2,1)S(1)} %get-tuple-element.177), channel_id=1, source_target_pairs={{0,3},{1,0},{2,1},{3,2},{4,7},{5,4},{6,5},{7,6},{8,11},{9,8},{10,9... | collective-permute-start | bytes 2359304 | tf_op jit(solution)/shard_map/ppermute | solution.py:149
  765.8 67.3 %collective-permute-start.31 = (bf16[256,1536]{1,0:T(8,128)(2,1)S(1)}, bf16[256,1536]{1,0:T(8,128)(2,1)S(1)}, u32[]{:S(2)}, u32[]{:S(2)}) collective-permute-start(bf16[256,1536]{1,0:T(8,128)(2,1)S(1)} %get-tuple-element.178), channel_id=1, source_target_pairs={{0,2},{1,3},{2,0},{3,1},{4,6},{5,7},{6,4},{7,5},{8,10},{9,11},{10,... | collective-permute-start | bytes 2359304 | tf_op jit(solution)/shard_map/ppermute | solution.py:149
  772.9 109.9 %collective-permute-start.24 = (bf16[256,1536]{1,0:T(8,128)(2,1)S(1)}, bf16[256,1536]{1,0:T(8,128)(2,1)S(1)}, u32[]{:S(2)}, u32[]{:S(2)}) collective-permute-start(bf16[256,1536]{1,0:T(8,128)(2,1)S(1)} %get-tuple-element.179), channel_id=1, source_target_pairs={{0,1},{1,2},{2,3},{3,0},{4,5},{5,6},{6,7},{7,4},{8,9},{9,10},{10,1... | collective-permute-start | bytes 2359304 | tf_op jit(solution)/shard_map/ppermute | solution.py:149
  773.9 111.8 %collective-permute-start.26 = (bf16[256,1536]{1,0:T(8,128)(2,1)S(1)}, bf16[256,1536]{1,0:T(8,128)(2,1)S(1)}, u32[]{:S(2)}, u32[]{:S(2)}) collective-permute-start(bf16[256,1536]{1,0:T(8,128)(2,1)S(1)} %get-tuple-element.180), channel_id=1, source_target_pairs={{0,3},{1,0},{2,1},{3,2},{4,7},{5,4},{6,5},{7,6},{8,11},{9,8},{10,9... | collective-permute-start | bytes 2359304 | tf_op jit(solution)/shard_map/ppermute | solution.py:149
  782.5 117.2 %collective-permute-start.25 = (bf16[256,1536]{1,0:T(8,128)(2,1)S(1)}, bf16[256,1536]{1,0:T(8,128)(2,1)S(1)}, u32[]{:S(2)}, u32[]{:S(2)}) collective-permute-start(bf16[256,1536]{1,0:T(8,128)(2,1)S(1)} %get-tuple-element.181), channel_id=1, source_target_pairs={{0,2},{1,3},{2,0},{3,1},{4,6},{5,7},{6,4},{7,5},{8,10},{9,11},{10,... | collective-permute-start | bytes 2359304 | tf_op jit(solution)/shard_map/ppermute | solution.py:149
  955.5 8.0 collective-permute-start.35
  956.9 12.2 %collective-permute-start.34 = (bf16[48,1536]{1,0:T(8,128)(2,1)S(1)}, bf16[48,1536]{1,0:T(8,128)(2,1)S(1)}, u32[]{:S(2)}, u32[]{:S(2)}) collective-permute-start(bf16[48,1536]{1,0:T(8,128)(2,1)S(1)} %get-tuple-element.228), channel_id=1, source_target_pairs={{0,2},{1,3},{2,0},{3,1},{4,6},{5,7},{6,4},{7,5},{8,10},{9,11},{10,... | collective-permute-start | bytes 442376 | tf_op jit(solution)/shard_map/ppermute | solution.py:149
  973.1 123.8 %collective-permute-start.39 = (bf16[128,1536]{1,0:T(8,128)(2,1)}, bf16[128,1536]{1,0:T(8,128)(2,1)S(1)}, u32[]{:S(2)}, u32[]{:S(2)}) collective-permute-start(bf16[128,1536]{1,0:T(8,128)(2,1)} %get-tuple-element.192), channel_id=1, source_target_pairs={{0,3},{1,0},{2,1},{3,2},{4,7},{5,4},{6,5},{7,6},{8,11},{9,8},{10,9... | collective-permute-start | bytes 1179656 | tf_op jit(solution)/shard_map/ppermute | solution.py:149
  974.5 124.0 %collective-permute-start.41 = (bf16[128,1536]{1,0:T(8,128)(2,1)}, bf16[128,1536]{1,0:T(8,128)(2,1)}, u32[]{:S(2)}, u32[]{:S(2)}) collective-permute-start(bf16[128,1536]{1,0:T(8,128)(2,1)} %get-tuple-element.193), channel_id=1, source_target_pairs={{0,1},{1,2},{2,3},{3,0},{4,5},{5,6},{6,7},{7,4},{8,9},{9,10},{10,1... | collective-permute-start | bytes 1179656 | tf_op jit(solution)/shard_map/ppermute | solution.py:149
  974.8 123.7 %collective-permute-start.40 = (bf16[128,1536]{1,0:T(8,128)(2,1)}, bf16[128,1536]{1,0:T(8,128)(2,1)}, u32[]{:S(2)}, u32[]{:S(2)}) collective-permute-start(bf16[128,1536]{1,0:T(8,128)(2,1)} %get-tuple-element.194), channel_id=1, source_target_pairs={{0,2},{1,3},{2,0},{3,1},{4,6},{5,7},{6,4},{7,5},{8,10},{9,11},{10,... | collective-permute-start | bytes 1179656 | tf_op jit(solution)/shard_map/ppermute | solution.py:149
  1094.6 18.3 %collective-permute-start.38 = (bf16[192,2048]{1,0:T(8,128)(2,1)S(1)}, bf16[192,2048]{1,0:T(8,128)(2,1)S(1)}, u32[]{:S(2)}, u32[]{:S(2)}) collective-permute-start(bf16[192,2048]{1,0:T(8,128)(2,1)S(1)} %bitcast.300), channel_id=1, source_target_pairs={{0,1},{1,2},{2,3},{3,0},{4,5},{5,6},{6,7},{7,4},{8,9},{9,10},{10,1... | collective-permute-start | bytes 2359304 | tf_op jit(solution)/shard_map/ppermute | solution.py:149
  1095.8 66.6 %collective-permute-start.37 = (bf16[192,2048]{1,0:T(8,128)(2,1)S(1)}, bf16[192,2048]{1,0:T(8,128)(2,1)S(1)}, u32[]{:S(2)}, u32[]{:S(2)}) collective-permute-start(bf16[192,2048]{1,0:T(8,128)(2,1)S(1)} %bitcast.299), channel_id=1, source_target_pairs={{0,2},{1,3},{2,0},{3,1},{4,6},{5,7},{6,4},{7,5},{8,10},{9,11},{10,... | collective-permute-start | bytes 2359304 | tf_op jit(solution)/shard_map/ppermute | solution.py:149
  1097.0 68.6 %collective-permute-start.36 = (bf16[192,2048]{1,0:T(8,128)(2,1)S(1)}, bf16[192,2048]{1,0:T(8,128)(2,1)S(1)}, u32[]{:S(2)}, u32[]{:S(2)}) collective-permute-start(bf16[192,2048]{1,0:T(8,128)(2,1)S(1)} %bitcast.298), channel_id=1, source_target_pairs={{0,3},{1,0},{2,1},{3,2},{4,7},{5,4},{6,5},{7,6},{8,11},{9,8},{10,9... | collective-permute-start | bytes 2359304 | tf_op jit(solution)/shard_map/ppermute | solution.py:149
  (91 other events, 1764.6 us)
Sparse Core Ops, SparseCore 0:
  10.1 37.0 all-gather.5
  49.1 38.7 all-gather.11
  118.3 131.2 all-gather.7
  323.0 73.2 all-gather.9
  710.9 51.4 reduce-scatter.4
  765.8 53.7 reduce-scatter.6
  823.1 92.6 reduce-scatter.10
  919.4 156.4 reduce-scatter.8

commit v2 on v1

v2 whole, which is shorter than its diff:
```python
import functools
import jax
import jax.numpy as jnp
from jax import lax
from jax.experimental import pallas as pl
from jax.experimental.pallas import tpu as pltpu
from jax.sharding import PartitionSpec as P

EPS = 1e-05
F32 = jnp.float32
BF16 = jnp.bfloat16
LANES = 128
TILE = 256
BIG = 2.0**100


def three_parts(value):
    high = value.astype(BF16).astype(F32)
    rest = value - high
    middle = rest.astype(BF16).astype(F32)
    return high, middle, rest - middle


def lane_pick(array, lane, index):
    return jnp.sum(jnp.where(lane == index, array, 0.0), axis=1, keepdims=True)


def with_extras(data, keep, place, extras):
    total = jnp.where(keep, data, 0.0)
    for index, extra in enumerate(extras):
        total = jnp.where(place == index, extra, total)
    return total.astype(BF16)


def nt(left, right):
    return lax.dot_general(left, right, (((1,), (1,)), ((), ())), preferred_element_type=F32)


def nn(left, right):
    return lax.dot_general(left, right, (((1,), (0,)), ((), ())), preferred_element_type=F32)


def head_sides(head, heads, size, side_ref):
    length = side_ref.shape[0]
    lane = lax.broadcasted_iota(jnp.int32, (length, LANES), 1)
    half = lax.rem(head, 2)
    keep = (lane >= half * size) & (lane < (half + 1) * size)
    place = lane - (1 - half) * size
    place = jnp.where(keep, -1, place)
    side = side_ref[...]
    decay = lane_pick(side, lane, head)
    segment = side[:, heads : heads + 1]
    padded = 1.0 - side[:, heads + 1 : heads + 2]
    return lane, keep, place, decay, segment, padded


def key_extras(decay, segment, padded):
    high, middle, low = three_parts(-decay)
    return [high, middle, low, segment, 1.0 - segment, padded, 1.0, 1.0, 1.0]


def query_extras(segment, total):
    return [1.0, 1.0, 1.0, -BIG * (1.0 - segment), -BIG * segment, -BIG] + list(
        three_parts(-total)
    )


PADDED_AT = 5


def forward_kernel(heads, size, scale, q_ref, k_ref, v_ref, side_ref, o_ref, total_ref, ks_ref):
    head = pl.program_id(0)
    length = q_ref.shape[0]
    lane, keep, place, decay, segment, padded = head_sides(head, heads, size, side_ref)
    ks_ref[...] = with_extras(k_ref[...].astype(F32), keep, place, key_extras(decay, segment, padded))

    @pl.when(head == 0)
    def _():
        total_ref[...] = jnp.zeros_like(total_ref)

    row = lax.broadcasted_iota(jnp.int32, (TILE, TILE), 0)
    column = lax.broadcasted_iota(jnp.int32, (TILE, TILE), 1)
    for first in range(0, length, TILE):
        here = pl.ds(first, TILE)
        part = slice(first, first + TILE)
        full = with_extras(
            q_ref[here, :].astype(F32) * scale, keep[part], place[part],
            query_extras(segment[part], 0.0 * segment[part]),
        )
        bare = jnp.where(place[part] == PADDED_AT, 0.0, full.astype(F32)).astype(BF16)
        keys = ks_ref[here, :]
        near = jnp.where(
            column < row, nt(full, keys), jnp.where(column == row, nt(bare, keys), -BIG)
        )
        highest = jnp.max(near, axis=1, keepdims=True)
        if first:
            far = nt(full, ks_ref[pl.ds(0, first), :])
            highest = jnp.maximum(highest, jnp.max(far, axis=1, keepdims=True))
        near = jnp.exp(near - highest)
        below = jnp.sum(near, axis=1, keepdims=True)
        mixed = nn(near.astype(BF16), v_ref[here, :])
        if first:
            far = jnp.exp(far - highest)
            below = below + jnp.sum(far, axis=1, keepdims=True)
            mixed = mixed + nn(far.astype(BF16), v_ref[pl.ds(0, first), :])
        mixed = (mixed / below).astype(BF16)
        o_ref[here, :] = jnp.where(keep[part], mixed, o_ref[here, :])
        total_ref[here, :] = jnp.where(
            lane[part] == head, highest + jnp.log(below), total_ref[here, :]
        )


def backward_kernel(
    heads, size, scale, q_ref, k_ref, v_ref, side_ref, total_ref, o_ref, g_ref,
    dq_ref, dk_ref, dv_ref, dd_ref, ks_ref, kt_ref, vs_ref, ak_ref, av_ref, row_ref,
):
    head = pl.program_id(0)
    length = q_ref.shape[0]
    lane, keep, place, decay, segment, padded = head_sides(head, heads, size, side_ref)
    keys = with_extras(k_ref[...].astype(F32), keep, place, key_extras(decay, segment, padded))
    ks_ref[...] = keys
    kt_ref[...] = keys.astype(F32).T.astype(BF16)
    vs_ref[...] = with_extras(v_ref[...].astype(F32), keep, place, [1.0, 1.0, 1.0])
    total = lane_pick(total_ref[...], lane, head)
    grads = jnp.where(keep, g_ref[...].astype(F32), 0.0)
    delta = jnp.sum(grads * o_ref[...].astype(F32), axis=1, keepdims=True)
    ak_ref[...] = jnp.zeros_like(ak_ref)
    av_ref[...] = jnp.zeros_like(av_ref)

    @pl.when(head == 0)
    def _():
        dd_ref[...] = jnp.zeros_like(dd_ref)

    row = lax.broadcasted_iota(jnp.int32, (TILE, TILE), 0)
    column = lax.broadcasted_iota(jnp.int32, (TILE, TILE), 1)
    for first in range(0, length, TILE):
        here = pl.ds(first, TILE)
        part = slice(first, first + TILE)
        full = with_extras(
            q_ref[here, :].astype(F32) * scale, keep[part], place[part],
            query_extras(segment[part], total[part]),
        )
        bare = jnp.where(place[part] == PADDED_AT, 0.0, full.astype(F32)).astype(BF16)
        grad = with_extras(grads[part], keep[part], place[part], three_parts(-delta[part]))
        spans = [(first, TILE)] + ([(0, first)] if first else [])
        grad_query = None
        for start, count in spans:
            span = pl.ds(start, count)
            scores = nt(ks_ref[span, :], full)
            if start == first:
                scores = jnp.where(
                    row < column, scores, jnp.where(row == column, nt(ks_ref[span, :], bare), -BIG)
                )
            probs = jnp.exp(scores)
            low = (probs * nt(vs_ref[span, :], grad)).astype(BF16)
            av_ref[span, :] += nn(probs.astype(BF16), grad)
            ak_ref[span, :] += nn(low, full)
            piece = nn(kt_ref[:, span], low)
            grad_query = piece if grad_query is None else grad_query + piece
        grad_query = grad_query.T
        dq_ref[here, :] = jnp.where(keep[part], (grad_query * scale).astype(BF16), dq_ref[here, :])
        row_ref[here, :] = grad_query
    dk_ref[...] = jnp.where(keep, ak_ref[...].astype(BF16), dk_ref[...])
    dv_ref[...] = jnp.where(keep, av_ref[...].astype(BF16), dv_ref[...])
    by_row = lane_pick(row_ref[...], place, 6)
    by_column = lane_pick(ak_ref[...], place, 0)
    dd_ref[...] = jnp.where(lane == head, by_row - by_column, dd_ref[...])


def specs_for(length, size, heads):
    def pair(offset):
        return pl.BlockSpec((length, LANES), lambda h: (0, offset * heads * size // LANES + h // 2))

    return pair, pl.BlockSpec((length, LANES), lambda h: (0, 0))


def make_side(decay, segment, present):
    length, heads = decay.shape
    side = jnp.concatenate(
        (decay, segment[:, None].astype(F32), present[:, None].astype(F32)), axis=1
    )
    return jnp.pad(side, ((0, 0), (0, LANES - heads - 2)))


def attention_forward(projected, side, heads, size):
    length = projected.shape[0]
    pair, whole = specs_for(length, size, heads)
    return pl.pallas_call(
        functools.partial(forward_kernel, heads, size, size ** (-0.5)),
        grid=(heads,),
        in_specs=[pair(0), pair(1), pair(2), whole],
        out_specs=[pair(0), whole],
        out_shape=[
            jax.ShapeDtypeStruct((length, heads * size), BF16),
            jax.ShapeDtypeStruct((length, LANES), F32),
        ],
        scratch_shapes=[pltpu.VMEM((length, LANES), BF16)],
    )(projected, projected, projected, side)


def attention_backward(projected, side, total, mixed, grad_mixed, heads, size):
    length = projected.shape[0]
    pair, whole = specs_for(length, size, heads)
    flat = jax.ShapeDtypeStruct((length, heads * size), BF16)
    return pl.pallas_call(
        functools.partial(backward_kernel, heads, size, size ** (-0.5)),
        grid=(heads,),
        in_specs=[pair(0), pair(1), pair(2), whole, whole, pair(0), pair(0)],
        out_specs=[pair(0), pair(0), pair(0), whole],
        out_shape=[flat, flat, flat, jax.ShapeDtypeStruct((length, LANES), F32)],
        scratch_shapes=[
            pltpu.VMEM((length, LANES), BF16),
            pltpu.VMEM((LANES, length), BF16),
            pltpu.VMEM((length, LANES), BF16),
            pltpu.VMEM((length, LANES), F32),
            pltpu.VMEM((length, LANES), F32),
            pltpu.VMEM((length, LANES), F32),
        ],
    )(projected, projected, projected, side, total, mixed, grad_mixed)


def rms_forward(rows, gain):
    inverse = lax.rsqrt(jnp.mean(rows * rows, axis=-1, keepdims=True) + EPS)
    return (rows * inverse * gain, inverse)


def rms_backward(rows, inverse, gain, upstream):
    scaled = upstream * gain
    return inverse * scaled - rows * inverse**3 * jnp.mean(scaled * rows, axis=-1, keepdims=True)


def dot(left, right, left_dim, right_dim):
    return lax.dot_general(
        left, right, (((left_dim,), (right_dim,)), ((), ())), preferred_element_type=F32
    )


def after(value, *others):
    return lax.optimization_barrier((value,) + others)[0]


def sum_everywhere(value, axes):
    for axis in axes:
        size = lax.axis_size(axis)
        if size & (size - 1):
            value = lax.psum(value, axis)
            continue
        step = 1
        while step < size:
            value = value + lax.ppermute(value, axis, [(i, i ^ step) for i in range(size)])
            step *= 2
    return value


def body(
    tokens,
    cotangent,
    segment_ids,
    slot_mask,
    attention_gain,
    query_weight,
    key_weight,
    value_weight,
    forget_weight,
    forget_bias,
    output_weight,
    swiglu_gain,
    gate_weight,
    up_weight,
    down_weight,
):
    batches, here, width = tokens.shape
    ranks = lax.axis_size("tensor")
    groups = lax.axis_size("dp")
    length = here * ranks
    heads_here = forget_weight.shape[1]
    head_width = query_weight.shape[1]
    head_size = head_width // heads_here
    units_here = gate_weight.shape[1]
    units = units_here * ranks
    unit_piece = down_weight.shape[0]
    head_piece = output_weight.shape[0]
    rank = lax.axis_index("tensor")
    bias_here = lax.dynamic_slice_in_dim(forget_bias, rank * heads_here, heads_here)

    def shift(value, step):
        if step % ranks == 0:
            return value
        return lax.ppermute(value, "tensor", [(i, (i + step) % ranks) for i in range(ranks)])

    def pieces_of(value):
        return [shift(value, step) for step in range(ranks)]

    def row_block(value, owner):
        return lax.dynamic_slice_in_dim(value, (owner % ranks) * here, here, 0)

    def place_rows(blocks, owners):
        total = jnp.zeros((length,) + blocks[0].shape[1:], blocks[0].dtype)
        for block, owner in zip(blocks, owners):
            total = lax.dynamic_update_slice_in_dim(total, block, (owner % ranks) * here, 0)
        return total

    mixed_in = jnp.concatenate((query_weight, key_weight, value_weight, forget_weight), axis=1)
    full_in = lax.all_gather(mixed_in, "dp", axis=0, tiled=True)
    row_pieces = pieces_of(jnp.concatenate((output_weight, down_weight), axis=0))
    pair_pieces = pieces_of(
        after(jnp.concatenate((gate_weight, up_weight), axis=1), *row_pieces)
    )
    full_rows = lax.all_gather(jnp.stack(row_pieces), "dp", axis=0)
    full_output = full_rows[:, :, :head_piece].transpose(1, 0, 2, 3)
    full_output = full_output.reshape(ranks * head_width, width)
    full_down = full_rows[:, :, head_piece:].reshape(units, width)

    def by_unit(blocks):
        split = [block.reshape(block.shape[0], groups, unit_piece) for block in blocks]
        return jnp.stack(split, axis=2).reshape(blocks[0].shape[0], units)

    pair_rows = jnp.concatenate(
        (
            by_unit([piece[:, :units_here] for piece in pair_pieces]),
            by_unit([piece[:, units_here:] for piece in pair_pieces]),
        ),
        axis=1,
    )
    full_pair = lax.all_gather(pair_rows, "dp", axis=0, tiled=True)

    rows = tokens.astype(F32)
    normed, inverse_one = rms_forward(rows, attention_gain)
    normed = normed.astype(BF16)
    saved = []
    mixed_parts = []
    previous = pair_pieces
    for batch in range(batches):
        normed_pieces = pieces_of(after(normed[batch], *previous))
        previous = normed_pieces
        normed_all = place_rows(normed_pieces, [rank - step + ranks for step in range(ranks)])
        projected = dot(normed_all, full_in[:, : 3 * head_width], 1, 0).astype(BF16)
        logits = dot(normed_all, full_in[:, 3 * head_width :], 1, 0) + bias_here
        decay = jnp.cumsum(jax.nn.log_sigmoid(logits), axis=0)
        side = make_side(decay, segment_ids[batch], slot_mask[batch])
        mixed, total = attention_forward(projected, side, heads_here, head_size)
        mixed_parts.append(
            jnp.concatenate(
                [shift(row_block(mixed, rank + step), step) for step in range(ranks)], axis=1
            )
        )
        saved.append((normed_all, projected, logits, side, total, mixed))

    mixed_here = jnp.concatenate(mixed_parts, axis=0)
    rows = rows.reshape(batches * here, width)
    upstream = cotangent.reshape(batches * here, width)
    hidden_state = rows + dot(mixed_here, full_output, 1, 0)
    normed_two, inverse_two = rms_forward(hidden_state, swiglu_gain)
    normed_two = normed_two.astype(BF16)
    both = dot(normed_two, full_pair, 1, 0)
    gate, upper = both[:, :units], both[:, units:]
    sigmoid_gate = jax.nn.sigmoid(gate)
    inner = (gate * sigmoid_gate * upper).astype(BF16)

    def scatter(value):
        return lax.psum_scatter(value, "dp", scatter_dimension=0, tiled=True)

    def settle(blocks):
        total = blocks[0].astype(F32)
        for step in range(1, ranks):
            total = total + shift(blocks[step], ranks - step).astype(F32)
        return total

    down_partial = dot(inner, upstream, 0, 0).astype(BF16)
    down_rows = scatter(down_partial)
    upstream_late = after(upstream, down_partial)
    grad_inner = dot(upstream_late, full_down, 1, 1)
    grad_both = jnp.concatenate(
        (
            (grad_inner * upper * sigmoid_gate * (1.0 + gate * (1.0 - sigmoid_gate))).astype(BF16),
            (grad_inner * gate * sigmoid_gate).astype(BF16),
        ),
        axis=1,
    )
    pair_partial = dot(normed_two, grad_both, 0, 0).astype(BF16)
    grad_normed_two = dot(after(grad_both, pair_partial), full_pair, 1, 1)
    gain_two = jnp.sum(grad_normed_two * hidden_state * inverse_two, axis=0)
    grad_hidden = upstream.astype(F32) + rms_backward(
        hidden_state, inverse_two, swiglu_gain, grad_normed_two
    )
    branch = grad_hidden.astype(BF16)
    pair_grad = scatter(after(pair_partial, down_rows, branch))
    grad_mixed_here = dot(branch, full_output, 1, 1).astype(BF16)
    inner_late, branch_late = lax.optimization_barrier((inner, branch, grad_mixed_here))[:2]
    layer_out = (hidden_state + dot(inner_late, full_down, 1, 0)).astype(BF16)
    output_partial = dot(mixed_here, branch_late, 0, 0).astype(BF16)
    output_partial = output_partial.reshape(ranks, groups, head_piece, width)
    output_partial = output_partial.transpose(1, 0, 2, 3).reshape(ranks * head_width, width)

    projected_grads = []
    bias_grad = jnp.zeros((heads_here,), F32)
    gain_one = jnp.zeros((width,), F32)
    grad_tokens = []
    for batch in range(batches):
        normed_all, projected, logits, side, total, mixed = saved[batch]
        part = grad_mixed_here[batch * here : (batch + 1) * here]
        blocks = [
            shift(part[:, step * head_width : (step + 1) * head_width], ranks - step)
            for step in range(ranks)
        ]
        grad_mixed = place_rows(blocks, [rank + step for step in range(ranks)])
        if batch + 1 == batches:
            grad_mixed = after(grad_mixed, down_rows, *projected_grads)
        grad_queries, grad_keys, grad_values, grad_decay = attention_backward(
            projected, side, total, mixed, grad_mixed, heads_here, head_size
        )
        carried = jnp.flip(jnp.cumsum(jnp.flip(grad_decay[:, :heads_here], 0), axis=0), 0)
        grad_logits = (carried * jax.nn.sigmoid(-logits)).astype(BF16)
        projected_grad = jnp.concatenate(
            (grad_queries, grad_keys, grad_values, grad_logits), axis=1
        )
        projected_grads.append(projected_grad)
        bias_grad = bias_grad + jnp.sum(grad_logits.astype(F32), axis=0)
        partial = dot(projected_grad, full_in, 1, 1).astype(BF16)
        grad_normed = row_block(partial, rank).astype(F32)
        for step in range(1, ranks):
            grad_normed = grad_normed + shift(row_block(partial, rank + step), step).astype(F32)
        own = rows[batch * here : (batch + 1) * here]
        gain_one = gain_one + jnp.sum(grad_normed * own * inverse_one[batch], axis=0)
        grad_tokens.append(
            grad_hidden[batch * here : (batch + 1) * here]
            + rms_backward(own, inverse_one[batch], attention_gain, grad_normed)
        )
    in_partial = dot(
        jnp.concatenate([item[0] for item in saved], axis=0),
        jnp.concatenate(projected_grads, axis=0),
        0,
        0,
    ).astype(BF16)
    last = scatter(after(jnp.concatenate((output_partial, in_partial), axis=1), pair_grad))
    in_grad = last[:, width:].astype(F32)

    down_rows = down_rows.reshape(ranks, unit_piece, width)
    down_grad = settle([down_rows[step] for step in range(ranks)])
    split = pair_grad.reshape(pair_grad.shape[0], 2, groups, ranks, unit_piece)
    pair_grad = settle(
        [split[:, :, :, step].reshape(pair_grad.shape[0], 2 * units_here) for step in range(ranks)]
    )
    output_rows = last[:, :width].reshape(ranks, head_piece, width)
    output_grad = settle([output_rows[step] for step in range(ranks)])
    bias_full = lax.dynamic_update_slice_in_dim(
        jnp.zeros(forget_bias.shape, F32), bias_grad, rank * heads_here, 0
    )
    sums = sum_everywhere(jnp.concatenate((gain_one, gain_two, bias_full)), ("dp", "tensor"))
    return (
        layer_out.reshape(batches, here, width),
        jnp.stack(grad_tokens),
        sums[:width],
        in_grad[:, :head_width],
        in_grad[:, head_width : 2 * head_width],
        in_grad[:, 2 * head_width : 3 * head_width],
        in_grad[:, 3 * head_width :],
        sums[2 * width :],
        output_grad,
        sums[width : 2 * width],
        pair_grad[:, :units_here],
        pair_grad[:, units_here:],
        down_grad,
    )


def solution(mesh):
    by_token = P(None, ("dp", "tensor"), None)
    by_column = P("dp", "tensor")
    by_row = P(("tensor", "dp"), None)
    weights = (by_column, by_column, by_column, by_column)
    return jax.shard_map(
        body,
        mesh=mesh,
        in_specs=(by_token, by_token, P(None, "dp"), P(None, "dp"), P())
        + weights
        + (P(), by_row, P(), by_column, by_column, by_row),
        out_specs=(by_token, by_token, P())
        + weights
        + (P(), by_row, P(), by_column, by_column, by_row),
        check_vma=False,
    )
```

time: 1190 us -> 1060 us (0.89)
  matrix products: 312 us -> 175 us
  Pallas kernels: 0 us -> 87.7 us
  local copies, waits for them, and re-layouts: 86.6 us -> 148 us
  waiting for transfers between devices: 530 us -> 481 us
  blocking collectives: 43 us -> 0 us
  other arithmetic: 111 us -> 75.2 us
  starting transfers between devices: 77.3 us -> 57.9 us
    dot_general x28 -> x0, matrix products: 147 us -> none  [the longest x8 66.8 us: block_scores(): jnp.einsum('qhd,khd->hqk', query_block, keys_all, preferred_element_type=...]
    reduce_scatter x4 -> x3, waiting for transfers between devices: 96.2 us -> 1.33 us  [scatter(): return lax.psum_scatter(value, 'dp', scatter_dimension=0, tiled=True)]
    pallas_call x0 -> x4, Pallas kernels: none -> 87.7 us  [the longest x2 52.3 us: attention_backward(): pl.pallas_call(functools.partial(backward_kernel, heads, size, size ** (-...]
    ppermute x42 -> x39, waiting for transfers between devices: 433 us -> 477 us  [shift(): lax.ppermute(value, 'tensor', [(i, (i + step) % ranks) for i in range(ran...]
    reduce_sum x6 -> x0, other arithmetic: 43.5 us -> none  [the longest x2 21 us: attention_backward(): jnp.sum(as_float, axis=-1)]
    psum x1 -> x0, blocking collectives: 43 us -> none  [body(): lax.psum((gain_one, gain_two, bias_full), ('dp', 'tensor'))]
    ppermute x42 -> x39, starting transfers between devices: 76.4 us -> 46.9 us  [shift(): lax.ppermute(value, 'tensor', [(i, (i + step) % ranks) for i in range(ran...]
    rev x4, local copies, waits for them, and re-layouts: 2.33 us -> 19.4 us  [the longest x2 9.9 us: body(): jnp.flip(jnp.cumsum(jnp.flip(grad_decay[:, :heads_here], 0), axis=0), 0)]
  transfers between devices with their start and end apart: 50 -> 50, of which waited for: 31 -> 29; matrix products, arithmetic and copies ran while one was open for 28% -> 33% of each run, Pallas kernels for 0% -> 8%
where the time goes in v2:
time: 1060 us; the launch traced here: 1040 us
  waiting for transfers between devices  481 us (45%)
  matrix products  175 us (17%)
  local copies, waits for them, and re-layouts  148 us (14%)
  Pallas kernels  87.7 us (8%)
  other arithmetic  75.2 us (7%)
  starting transfers between devices  57.9 us (5%)
  between operations  15.1 us (1%)
    ppermute x39, waiting for transfers between devices, shift(): lax.ppermute(value, 'tensor', [(i, (i + step) % ranks) for i in range(ran...  477 us
    dot_general x16, matrix products, dot(): lax.dot_general(left, right, (((left_dim,), (right_dim,)), ((), ())), pre...  175 us
    pallas_call x2, Pallas kernels, attention_backward(): pl.pallas_call(functools.partial(backward_kernel, heads, size, size ** (-...  52.3 us
    ppermute x39, starting transfers between devices, shift(): lax.ppermute(value, 'tensor', [(i, (i + step) % ranks) for i in range(ran...  46.9 us
    pallas_call x2, Pallas kernels, attention_forward(): pl.pallas_call(functools.partial(forward_kernel, heads, size, size ** (-0...  35.4 us
  transfers between devices with their start and end apart: 50, of which 29 were waited for; matrix products, arithmetic and copies ran while one was open for 33% of the time, Pallas kernels for 8%

profile of v2, /device:TPU:9, one launch (start us, length us, event | category | flops | bytes accessed | tf_op | source)
XLA Modules:
  0.0 1040.2 jit_solution(6478665917441411738)
XLA Ops:
  15.8 9.5 collective-permute-done
  25.3 33.8 %collective-permute-done.1 = bf16[176,1536]{1,0:T(8,128)(2,1)S(1)} collective-permute-done((bf16[176,1536]{1,0:T(8,128)(2,1)S(1)}, bf16[176,1536]{1,0:T(8,128)(2,1)S(1)}, u32[]{:S(2)}, u32[]{:S(2)}) %collective-permute-start.1) | collective-permute-done | bytes 540704 | tf_op jit(solution)/shard_map/ppermute | solution.py:289
  67.5 14.9 %collective-permute-done.3 = bf16[192,2048]{1,0:T(8,128)(2,1)} collective-permute-done((bf16[192,2048]{1,0:T(8,128)(2,1)S(1)}, bf16[192,2048]{1,0:T(8,128)(2,1)}, u32[]{:S(2)}, u32[]{:S(2)}) %collective-permute-start.3) | collective-permute-done | bytes 786464 | tf_op jit(solution)/shard_map/ppermute | solution.py:289
  84.0 47.0 %collective-permute-done.4 = bf16[192,2048]{1,0:T(8,128)(2,1)} collective-permute-done((bf16[192,2048]{1,0:T(8,128)(2,1)S(1)}, bf16[192,2048]{1,0:T(8,128)(2,1)}, u32[]{:S(2)}, u32[]{:S(2)}) %collective-permute-start.4) | collective-permute-done | bytes 786464 | tf_op jit(solution)/shard_map/ppermute | solution.py:289
  138.0 4.8 pad_maximum_fusion.6
  151.3 5.0 pad_maximum_fusion.7
  177.1 6.9 collective-permute-done.6
  184.0 48.6 %collective-permute-done.7 = bf16[256,1536]{1,0:T(8,128)(2,1)} collective-permute-done((bf16[256,1536]{1,0:T(8,128)(2,1)}, bf16[256,1536]{1,0:T(8,128)(2,1)}, u32[]{:S(2)}, u32[]{:S(2)}) %collective-permute-start.7) | collective-permute-done | bytes 786464 | tf_op jit(solution)/shard_map/ppermute | solution.py:289
  232.7 22.0 %collective-permute-done.8 = bf16[256,1536]{1,0:T(8,128)(2,1)} collective-permute-done((bf16[256,1536]{1,0:T(8,128)(2,1)}, bf16[256,1536]{1,0:T(8,128)(2,1)}, u32[]{:S(2)}, u32[]{:S(2)}) %collective-permute-start.8) | collective-permute-done | bytes 786464 | tf_op jit(solution)/shard_map/ppermute | solution.py:289
  265.3 8.1 collective-permute-done.12
  274.3 47.6 %collective-permute-done.13 = bf16[256,1536]{1,0:T(8,128)(2,1)S(1)} collective-permute-done((bf16[256,1536]{1,0:T(8,128)(2,1)S(1)}, bf16[256,1536]{1,0:T(8,128)(2,1)S(1)}, u32[]{:S(2)}, u32[]{:S(2)}) %collective-permute-start.13) | collective-permute-done | bytes 786464 | tf_op jit(solution)/shard_map/ppermute | solution.py:289
  341.3 8.6 convolution_convert_fusion.5.q_ref.k_ref.v_ref
  349.9 17.7 %shard_map.246 = (bf16[1024,384]{1,0:T(8,128)(2,1)}, f32[1024,128]{1,0:T(8,128)}) custom-call(bf16[1024,1152]{1,0:T(8,128)(2,1)} %convolution_convert_fusion.5.q_ref.k_ref.v_ref, bf16[1024,1152]{1,0:T(8,128)(2,1)} %convolution_convert_fusion.5.q_ref.k_ref.v_ref, bf16[1024,1152]{1,0:T(8,128)(2,1)} %convolution_convert_fusion.5.q_ref.k_ref.v_ref, ...), custom_call_target="tpu_custom_call" | custom-call | tf_op jit(solution)/shard_map/pallas_call | solution.py:188
  374.2 8.6 convolution_convert_fusion.4.q_ref.k_ref.v_ref
  385.7 17.7 %shard_map.247 = (bf16[1024,384]{1,0:T(8,128)(2,1)}, f32[1024,128]{1,0:T(8,128)}) custom-call(bf16[1024,1152]{1,0:T(8,128)(2,1)} %convolution_convert_fusion.4.q_ref.k_ref.v_ref, bf16[1024,1152]{1,0:T(8,128)(2,1)} %convolution_convert_fusion.4.q_ref.k_ref.v_ref, bf16[1024,1152]{1,0:T(8,128)(2,1)} %convolution_convert_fusion.4.q_ref.k_ref.v_ref, ...), custom_call_target="tpu_custom_call" | custom-call | tf_op jit(solution)/shard_map/pallas_call | solution.py:188
  411.9 9.0 collective-permute-done.16
  421.0 4.8 collective-permute-done.17
  425.8 5.6 multiply_reduce_fusion.2
  432.0 22.2 %fusion.47 = f32[512,8192]{1,0:T(8,128)} fusion(bf16[1536,8192]{1,0:T(8,128)(2,1)} %all-gather.7.cloned.1.call-done, f32[512,1536]{1,0:T(8,128)} %get-tuple-element.202, f32[1536]{0:T(1024)S(1)} %copy-done.28, f32[512]{0:T(512)S(1)} %get-tuple-element.196), kind=kOutput, calls=%fused_computation.174 | convolution fusion | flops 12887261184 | bytes 45096960 | tf_op jit(solution)/shard_map/dot_general | solution.py:233
  454.2 7.2 multiply_convert_fusion.2
  463.4 9.7 convolution_convert_fusion.1
  473.6 11.7 %slice.316 = bf16[8,4,128,1536]{3,2,1,0:T(8,128)(2,1)} slice(bf16[8,4,176,1536]{3,2,1,0:T(8,128)(2,1)} %bitcast.165), slice={[0:8], [0:4], [48:176], [0:1536]} | slice | bytes 25165824 | tf_op jit(solution)/shard_map/slice | solution.py:312
  485.3 23.9 %multiply_convert_fusion.1 = (bf16[512,4096]{1,0:T(8,128)(2,1)}, bf16[512,4096]{1,0:T(8,128)(2,1)}) fusion(f32[512,8192]{1,0:T(8,128)} %fusion.47, bf16[512,1536]{1,0:T(8,128)(2,1)S(1)} %bitcast.182, bf16[4096,1536]{1,0:T(8,128)(2,1)} %bitcast.166), kind=kOutput, calls=%fused_computation.5 | convolution fusion | flops 6469713920 | bytes 39321600 | tf_op jit(solution)/shard_map/dot_general | solution.py:233
  509.2 7.8 pad_maximum_fusion.1
  517.1 20.9 %convolution_convert_fusion = bf16[1536,8192]{1,0:T(8,128)(2,1)} fusion(f32[512,1536]{1,0:T(8,128)S(1)} %copy-done.9, f32[1536]{0:T(1024)S(1)} %copy-done.28, f32[512]{0:T(512)S(1)} %get-tuple-element.196, bf16[512,4096]{1,0:T(8,128)(2,1)} %get-tuple-element.142, bf16[512,4096]{1,0:T(8,128)(2,1)} %get-tuple-element.141), kind=kOutput, calls=%fused_computation | convolution fusion | flops 12916621312 | bytes 36708352 | tf_op jit(solution)/shard_map/dot_general | solution.py:233
  538.0 21.1 %multiply_reduce_fusion = (f32[1536]{0:T(1024)S(1)}, f32[512]{0:T(512)S(1)}, f32[512,1536]{1,0:T(8,128)}) fusion(f32[512,1536]{1,0:T(8,128)S(1)} %copy-done.9, f32[512]{0:T(512)} %copy-done.30, f32[1536]{0:T(1024)S(1)} %copy-done.28, bf16[512,8192]{1,0:T(8,128)(2,1)} %pad_maximum_fusion.1, bf16[1536,8192]{1,0:T(8,128)(2,1)} %all-gather.7.cloned.1.call-done), kind=kOutput, calls=%fused_computation.37 | convolution fusion | flops 12889618432 | bytes 39862272 | tf_op jit(solution)/shard_map/dot_general | solution.py:233
  564.6 5.6 convolution_convert_fusion.8
  585.8 23.9 %collective-permute-done.18 = bf16[256,384]{1,0:T(8,128)(2,1)S(1)} collective-permute-done((bf16[256,384]{1,0:T(8,128)(2,1)S(1)}, bf16[256,384]{1,0:T(8,128)(2,1)S(1)}, u32[]{:S(2)}, u32[]{:S(2)}) %collective-permute-start.18) | collective-permute-done | bytes 196640 | tf_op jit(solution)/shard_map/ppermute | solution.py:289
  615.3 26.3 %shard_map.248 = (bf16[1024,384]{1,0:T(8,128)(2,1)}, bf16[1024,384]{1,0:T(8,128)(2,1)}, bf16[1024,384]{1,0:T(8,128)(2,1)}, f32[1024,128]{1,0:T(8,128)}) custom-call(bf16[1024,1152]{1,0:T(8,128)(2,1)} %convolution_convert_fusion.5.q_ref.k_ref.v_ref, bf16[1024,1152]{1,0:T(8,128)(2,1)} %convolution_convert_fusion.5.q_ref.k_ref.v_ref, ...), custom_call_target="tpu_custom_call" | custom-call | tf_op jit(solution)/shard_map/pallas_call | solution.py:205
  641.6 4.8 rev.13
  661.9 26.0 %shard_map.249 = (bf16[1024,384]{1,0:T(8,128)(2,1)}, bf16[1024,384]{1,0:T(8,128)(2,1)}, bf16[1024,384]{1,0:T(8,128)(2,1)}, f32[1024,128]{1,0:T(8,128)}) custom-call(bf16[1024,1152]{1,0:T(8,128)(2,1)} %convolution_convert_fusion.4.q_ref.k_ref.v_ref, bf16[1024,1152]{1,0:T(8,128)(2,1)} %convolution_convert_fusion.4.q_ref.k_ref.v_ref, ...), custom_call_target="tpu_custom_call" | custom-call | tf_op jit(solution)/shard_map/pallas_call | solution.py:205
  687.9 4.8 rev.15
  697.0 5.1 rev.16
  704.4 13.9 %convolution_convert_fusion.3 = bf16[1536,1158]{0,1:T(8,128)(2,1)} fusion(bf16[1024,1536]{1,0:T(8,128)(2,1)} %constant_dynamic-update-slice_fusion.6, bf16[1024,1536]{1,0:T(8,128)(2,1)} %constant_dynamic-update-slice_fusion.10, bf16[1024,6]{1,0:T(8,128)(2,1)S(1)} %get-tuple-element.134, bf16[1024,384]{1,0:T(8,128)(2,1)} %get-tuple-element.52, ...), kind=kOutput, calls=%fused_computation.9 | convolution fusion | flops 7337812992 | bytes 14592000 | tf_op jit(solution)/shard_map/dot_general | solution.py:233
  718.3 6.1 copy.150
  724.4 7.6 pad_maximum_fusion
  732.6 7.2 convolution_convert_fusion.7
  748.3 8.3 convolution_convert_fusion.6
  765.2 7.8 fusion.20
  773.2 37.8 %collective-permute-done.22 = bf16[256,1536]{1,0:T(8,128)(2,1)} collective-permute-done((bf16[256,1536]{1,0:T(8,128)(2,1)}, bf16[256,1536]{1,0:T(8,128)(2,1)}, u32[]{:S(2)}, u32[]{:S(2)}) %collective-permute-start.22) | collective-permute-done | bytes 786464 | tf_op jit(solution)/shard_map/ppermute | solution.py:289
  811.0 38.3 %collective-permute-done.23 = bf16[256,1536]{1,0:T(8,128)(2,1)} collective-permute-done((bf16[256,1536]{1,0:T(8,128)(2,1)}, bf16[256,1536]{1,0:T(8,128)(2,1)}, u32[]{:S(2)}, u32[]{:S(2)}) %collective-permute-start.23) | collective-permute-done | bytes 786464 | tf_op jit(solution)/shard_map/ppermute | solution.py:289
  849.3 27.9 %collective-permute-done.27 = bf16[256,1536]{1,0:T(8,128)(2,1)} collective-permute-done((bf16[256,1536]{1,0:T(8,128)(2,1)}, bf16[256,1536]{1,0:T(8,128)(2,1)}, u32[]{:S(2)}, u32[]{:S(2)}) %collective-permute-start.27) | collective-permute-done | bytes 786464 | tf_op jit(solution)/shard_map/ppermute | solution.py:289
  879.6 14.4 %collective-permute-done.28 = bf16[256,1536]{1,0:T(8,128)(2,1)} collective-permute-done((bf16[256,1536]{1,0:T(8,128)(2,1)S(1)}, bf16[256,1536]{1,0:T(8,128)(2,1)}, u32[]{:S(2)}, u32[]{:S(2)}) %collective-permute-start.28) | collective-permute-done | bytes 786464 | tf_op jit(solution)/shard_map/ppermute | solution.py:289
  894.0 5.9 collective-permute-done.29
  917.2 7.0 collective-permute-start.33
  931.4 13.3 %slice_reduce_fusion.2 = (bf16[192,2,8,128]{3,2,1,0:T(8,128)(2,1)S(1)}, bf16[192,2,8,128]{3,2,1,0:T(8,128)(2,1)S(1)}, bf16[192,2,8,128]{3,2,1,0:T(8,128)(2,1)S(1)}) fusion(bf16[192,2,8,4,128]{4,3,2,1,0:T(4,128)(2,1)S(1)} %reshape.272), kind=kLoop, calls=%fused_computation.62 | loop fusion | bytes 4718592 | tf_op jit(solution)/shard_map/slice | solution.py:442
  960.5 37.6 %collective-permute-done.39 = bf16[192,2048]{1,0:T(8,128)(2,1)S(1)} collective-permute-done((bf16[192,2048]{1,0:T(8,128)(2,1)S(1)}, bf16[192,2048]{1,0:T(8,128)(2,1)S(1)}, u32[]{:S(2)}, u32[]{:S(2)}) %collective-permute-start.39) | collective-permute-done | bytes 786464 | tf_op jit(solution)/shard_map/ppermute | solution.py:289
  998.1 16.9 %collective-permute-done.40 = bf16[192,2048]{1,0:T(8,128)(2,1)S(1)} collective-permute-done((bf16[192,2048]{1,0:T(8,128)(2,1)S(1)}, bf16[192,2048]{1,0:T(8,128)(2,1)S(1)}, u32[]{:S(2)}, u32[]{:S(2)}) %collective-permute-start.40) | collective-permute-done | bytes 786464 | tf_op jit(solution)/shard_map/ppermute | solution.py:289
  (288 shorter events, 234.0 us)
Async XLA Ops:
  7.2 316.6 %all-gather.5.cloned.1.call-start = ((), (), s32[]{:S(2)}) async-start(), calls=%async_computation.3 | async-start | bytes 4423680 | tf_op jit(solution)/shard_map/all_gather | solution.py:304
  10.0 398.9 %all-gather.9.cloned.1.call-start = ((), (), s32[]{:S(2)}) async-start(), calls=%async_computation.8 | async-start | bytes 19464192 | tf_op jit(solution)/shard_map/all_gather | solution.py:309
  12.0 13.3 %collective-permute-start = (bf16[176,1536]{1,0:T(8,128)(2,1)S(1)}, bf16[176,1536]{1,0:T(8,128)(2,1)S(1)}, u32[]{:S(2)}, u32[]{:S(2)}) collective-permute-start(bf16[176,1536]{1,0:T(8,128)(2,1)S(1)} %constant_dynamic-update-slice_fusion.14), channel_id=1, source_target_pairs={{0,1},{1,2},{2,3},{3,0},{4,5},{5,6},{6,7},{7,4},{8,9},{9,10},{10,1... | collective-permute-start | bytes 1622024 | tf_op jit(solution)/shard_map/ppermute | solution.py:289
  13.3 45.7 %collective-permute-start.1 = (bf16[176,1536]{1,0:T(8,128)(2,1)S(1)}, bf16[176,1536]{1,0:T(8,128)(2,1)S(1)}, u32[]{:S(2)}, u32[]{:S(2)}) collective-permute-start(bf16[176,1536]{1,0:T(8,128)(2,1)S(1)} %constant_dynamic-update-slice_fusion.14), channel_id=1, source_target_pairs={{0,2},{1,3},{2,0},{3,1},{4,6},{5,7},{6,4},{7,5},{8,10},{9,11},{10,... | collective-permute-start | bytes 1622024 | tf_op jit(solution)/shard_map/ppermute | solution.py:289
  14.4 47.5 %collective-permute-start.2 = (bf16[176,1536]{1,0:T(8,128)(2,1)S(1)}, bf16[176,1536]{1,0:T(8,128)(2,1)S(1)}, u32[]{:S(2)}, u32[]{:S(2)}) collective-permute-start(bf16[176,1536]{1,0:T(8,128)(2,1)S(1)} %constant_dynamic-update-slice_fusion.14), channel_id=1, source_target_pairs={{0,3},{1,0},{2,1},{3,2},{4,7},{5,4},{6,5},{7,6},{8,11},{9,8},{10,9... | collective-permute-start | bytes 1622024 | tf_op jit(solution)/shard_map/ppermute | solution.py:289
  63.5 368.5 %all-gather.7.cloned.1.call-start = ((), (), s32[]{:S(2)}) async-start(), calls=%async_computation.4 | async-start | bytes 28311552 | tf_op jit(solution)/shard_map/all_gather | solution.py:325
  63.7 18.8 %collective-permute-start.3 = (bf16[192,2048]{1,0:T(8,128)(2,1)S(1)}, bf16[192,2048]{1,0:T(8,128)(2,1)}, u32[]{:S(2)}, u32[]{:S(2)}) collective-permute-start(bf16[192,2048]{1,0:T(8,128)(2,1)S(1)} %pad_maximum_fusion.8), channel_id=1, source_target_pairs={{0,1},{1,2},{2,3},{3,0},{4,5},{5,6},{6,7},{7,4},{8,9},{9,10},{10,1... | collective-permute-start | bytes 2359304 | tf_op jit(solution)/shard_map/ppermute | solution.py:289
  63.8 67.2 %collective-permute-start.4 = (bf16[192,2048]{1,0:T(8,128)(2,1)S(1)}, bf16[192,2048]{1,0:T(8,128)(2,1)}, u32[]{:S(2)}, u32[]{:S(2)}) collective-permute-start(bf16[192,2048]{1,0:T(8,128)(2,1)S(1)} %pad_maximum_fusion.8), channel_id=1, source_target_pairs={{0,2},{1,3},{2,0},{3,1},{4,6},{5,7},{6,4},{7,5},{8,10},{9,11},{10,... | collective-permute-start | bytes 2359304 | tf_op jit(solution)/shard_map/ppermute | solution.py:289
  64.1 70.4 %collective-permute-start.5 = (bf16[192,2048]{1,0:T(8,128)(2,1)S(1)}, bf16[192,2048]{1,0:T(8,128)(2,1)}, u32[]{:S(2)}, u32[]{:S(2)}) collective-permute-start(bf16[192,2048]{1,0:T(8,128)(2,1)S(1)} %pad_maximum_fusion.8), channel_id=1, source_target_pairs={{0,3},{1,0},{2,1},{3,2},{4,7},{5,4},{6,5},{7,6},{8,11},{9,8},{10,9... | collective-permute-start | bytes 2359304 | tf_op jit(solution)/shard_map/ppermute | solution.py:289
  162.1 402.4 %reduce-scatter.4.cloned.1.call-start = ((), (), s32[]{:S(2)}) async-start(), calls=%async_computation.5 | async-start | bytes 14155776 | tf_op jit(solution)/shard_map/reduce_scatter | solution.py:361
  165.6 18.4 %collective-permute-start.6 = (bf16[256,1536]{1,0:T(8,128)(2,1)}, bf16[256,1536]{1,0:T(8,128)(2,1)}, u32[]{:S(2)}, u32[]{:S(2)}) collective-permute-start(bf16[256,1536]{1,0:T(8,128)(2,1)} %get-tuple-element.36), channel_id=1, source_target_pairs={{0,1},{1,2},{2,3},{3,0},{4,5},{5,6},{6,7},{7,4},{8,9},{9,10},{10,1... | collective-permute-start | bytes 2359304 | tf_op jit(solution)/shard_map/ppermute | solution.py:289
  165.7 67.0 %collective-permute-start.7 = (bf16[256,1536]{1,0:T(8,128)(2,1)}, bf16[256,1536]{1,0:T(8,128)(2,1)}, u32[]{:S(2)}, u32[]{:S(2)}) collective-permute-start(bf16[256,1536]{1,0:T(8,128)(2,1)} %get-tuple-element.36), channel_id=1, source_target_pairs={{0,2},{1,3},{2,0},{3,1},{4,6},{5,7},{6,4},{7,5},{8,10},{9,11},{10,... | collective-permute-start | bytes 2359304 | tf_op jit(solution)/shard_map/ppermute | solution.py:289
  169.0 85.7 %collective-permute-start.8 = (bf16[256,1536]{1,0:T(8,128)(2,1)}, bf16[256,1536]{1,0:T(8,128)(2,1)}, u32[]{:S(2)}, u32[]{:S(2)}) collective-permute-start(bf16[256,1536]{1,0:T(8,128)(2,1)} %get-tuple-element.36), channel_id=1, source_target_pairs={{0,3},{1,0},{2,1},{3,2},{4,7},{5,4},{6,5},{7,6},{8,11},{9,8},{10,9... | collective-permute-start | bytes 2359304 | tf_op jit(solution)/shard_map/ppermute | solution.py:289
  254.7 18.7 %collective-permute-start.12 = (bf16[256,1536]{1,0:T(8,128)(2,1)S(1)}, bf16[256,1536]{1,0:T(8,128)(2,1)S(1)}, u32[]{:S(2)}, u32[]{:S(2)}) collective-permute-start(bf16[256,1536]{1,0:T(8,128)(2,1)S(1)} %copy-done.8), channel_id=1, source_target_pairs={{0,1},{1,2},{2,3},{3,0},{4,5},{5,6},{6,7},{7,4},{8,9},{9,10},{10,1... | collective-permute-start | bytes 2359304 | tf_op jit(solution)/shard_map/ppermute | solution.py:289
  254.7 67.2 %collective-permute-start.13 = (bf16[256,1536]{1,0:T(8,128)(2,1)S(1)}, bf16[256,1536]{1,0:T(8,128)(2,1)S(1)}, u32[]{:S(2)}, u32[]{:S(2)}) collective-permute-start(bf16[256,1536]{1,0:T(8,128)(2,1)S(1)} %copy-done.8), channel_id=1, source_target_pairs={{0,2},{1,3},{2,0},{3,1},{4,6},{5,7},{6,4},{7,5},{8,10},{9,11},{10,... | collective-permute-start | bytes 2359304 | tf_op jit(solution)/shard_map/ppermute | solution.py:289
  254.7 68.2 %collective-permute-start.14 = (bf16[256,1536]{1,0:T(8,128)(2,1)S(1)}, bf16[256,1536]{1,0:T(8,128)(2,1)S(1)}, u32[]{:S(2)}, u32[]{:S(2)}) collective-permute-start(bf16[256,1536]{1,0:T(8,128)(2,1)S(1)} %copy-done.8), channel_id=1, source_target_pairs={{0,3},{1,0},{2,1},{3,2},{4,7},{5,4},{6,5},{7,6},{8,11},{9,8},{10,9... | collective-permute-start | bytes 2359304 | tf_op jit(solution)/shard_map/ppermute | solution.py:289
  369.6 37.9 %collective-permute-start.10 = (bf16[256,384]{1,0:T(8,128)(2,1)}, bf16[256,384]{1,0:T(8,128)(2,1)}, u32[]{:S(2)}, u32[]{:S(2)}) collective-permute-start(bf16[256,384]{1,0:T(8,128)(2,1)} %get-tuple-element.181), channel_id=1, source_target_pairs={{0,2},{1,3},{2,0},{3,1},{4,6},{5,7},{6,4},{7,5},{8,10},{9,11},{10,... | collective-permute-start | bytes 589832 | tf_op jit(solution)/shard_map/ppermute | solution.py:289
  372.7 39.2 %collective-permute-start.11 = (bf16[256,384]{1,0:T(8,128)(2,1)}, bf16[256,384]{1,0:T(8,128)(2,1)}, u32[]{:S(2)}, u32[]{:S(2)}) collective-permute-start(bf16[256,384]{1,0:T(8,128)(2,1)} %get-tuple-element.180), channel_id=1, source_target_pairs={{0,3},{1,0},{2,1},{3,2},{4,7},{5,4},{6,5},{7,6},{8,11},{9,8},{10,9... | collective-permute-start | bytes 589832 | tf_op jit(solution)/shard_map/ppermute | solution.py:289
  372.7 39.2 %collective-permute-start.9 = (bf16[256,384]{1,0:T(8,128)(2,1)}, bf16[256,384]{1,0:T(8,128)(2,1)}, u32[]{:S(2)}, u32[]{:S(2)}) collective-permute-start(bf16[256,384]{1,0:T(8,128)(2,1)} %get-tuple-element.182), channel_id=1, source_target_pairs={{0,1},{1,2},{2,3},{3,0},{4,5},{5,6},{6,7},{7,4},{8,9},{9,10},{10,1... | collective-permute-start | bytes 589832 | tf_op jit(solution)/shard_map/ppermute | solution.py:289
  405.4 6.6 collective-permute-start.15
  405.4 15.6 %collective-permute-start.16 = (bf16[256,384]{1,0:T(8,128)(2,1)}, bf16[256,384]{1,0:T(8,128)(2,1)}, u32[]{:S(2)}, u32[]{:S(2)}) collective-permute-start(bf16[256,384]{1,0:T(8,128)(2,1)} %get-tuple-element.185), channel_id=1, source_target_pairs={{0,2},{1,3},{2,0},{3,1},{4,6},{5,7},{6,4},{7,5},{8,10},{9,11},{10,... | collective-permute-start | bytes 589832 | tf_op jit(solution)/shard_map/ppermute | solution.py:289
  407.5 18.3 %collective-permute-start.17 = (bf16[256,384]{1,0:T(8,128)(2,1)}, bf16[256,384]{1,0:T(8,128)(2,1)}, u32[]{:S(2)}, u32[]{:S(2)}) collective-permute-start(bf16[256,384]{1,0:T(8,128)(2,1)} %get-tuple-element.184), channel_id=1, source_target_pairs={{0,3},{1,0},{2,1},{3,2},{4,7},{5,4},{6,5},{7,6},{8,11},{9,8},{10,9... | collective-permute-start | bytes 589832 | tf_op jit(solution)/shard_map/ppermute | solution.py:289
  473.1 258.8 %reduce-scatter.6.cloned.1.call-start = ((), (), s32[]{:S(2)}) async-start(), calls=%async_computation.6 | async-start | bytes 28311552 | tf_op jit(solution)/shard_map/reduce_scatter | solution.py:361
  564.6 452.5 %reduce-scatter.8.cloned.1.call-start = ((), (), s32[]{:S(2)}) async-start(), calls=%async_computation.7 | async-start | bytes 9732096 | tf_op jit(solution)/shard_map/reduce_scatter | solution.py:361
  578.5 77.0 %collective-permute-start.24 = (bf16[256,384]{1,0:T(8,128)(2,1)}, bf16[256,384]{1,0:T(8,128)(2,1)}, u32[]{:S(2)}, u32[]{:S(2)}) collective-permute-start(bf16[256,384]{1,0:T(8,128)(2,1)} %get-tuple-element.158), channel_id=1, source_target_pairs={{0,3},{1,0},{2,1},{3,2},{4,7},{5,4},{6,5},{7,6},{8,11},{9,8},{10,9... | collective-permute-start | bytes 589832 | tf_op jit(solution)/shard_map/ppermute | solution.py:289
  578.7 78.5 %collective-permute-start.25 = (bf16[256,384]{1,0:T(8,128)(2,1)}, bf16[256,384]{1,0:T(8,128)(2,1)}, u32[]{:S(2)}, u32[]{:S(2)}) collective-permute-start(bf16[256,384]{1,0:T(8,128)(2,1)} %get-tuple-element.157), channel_id=1, source_target_pairs={{0,2},{1,3},{2,0},{3,1},{4,6},{5,7},{6,4},{7,5},{8,10},{9,11},{10,... | collective-permute-start | bytes 589832 | tf_op jit(solution)/shard_map/ppermute | solution.py:289
  580.8 78.0 %collective-permute-start.26 = (bf16[256,384]{1,0:T(8,128)(2,1)S(1)}, bf16[256,384]{1,0:T(8,128)(2,1)}, u32[]{:S(2)}, u32[]{:S(2)}) collective-permute-start(bf16[256,384]{1,0:T(8,128)(2,1)S(1)} %get-tuple-element.156), channel_id=1, source_target_pairs={{0,1},{1,2},{2,3},{3,0},{4,5},{5,6},{6,7},{7,4},{8,9},{9,10},{10,1... | collective-permute-start | bytes 589832 | tf_op jit(solution)/shard_map/ppermute | solution.py:289
  583.0 26.7 %collective-permute-start.18 = (bf16[256,384]{1,0:T(8,128)(2,1)S(1)}, bf16[256,384]{1,0:T(8,128)(2,1)S(1)}, u32[]{:S(2)}, u32[]{:S(2)}) collective-permute-start(bf16[256,384]{1,0:T(8,128)(2,1)S(1)} %get-tuple-element.162), channel_id=1, source_target_pairs={{0,3},{1,0},{2,1},{3,2},{4,7},{5,4},{6,5},{7,6},{8,11},{9,8},{10,9... | collective-permute-start | bytes 589832 | tf_op jit(solution)/shard_map/ppermute | solution.py:289
  583.0 27.4 %collective-permute-start.19 = (bf16[256,384]{1,0:T(8,128)(2,1)S(1)}, bf16[256,384]{1,0:T(8,128)(2,1)S(1)}, u32[]{:S(2)}, u32[]{:S(2)}) collective-permute-start(bf16[256,384]{1,0:T(8,128)(2,1)S(1)} %get-tuple-element.161), channel_id=1, source_target_pairs={{0,2},{1,3},{2,0},{3,1},{4,6},{5,7},{6,4},{7,5},{8,10},{9,11},{10,... | collective-permute-start | bytes 589832 | tf_op jit(solution)/shard_map/ppermute | solution.py:289
  609.7 4.9 collective-permute-start.20
  742.8 18.3 %collective-permute-start.21 = (bf16[256,1536]{1,0:T(8,128)(2,1)S(1)}, bf16[256,1536]{1,0:T(8,128)(2,1)S(1)}, u32[]{:S(2)}, u32[]{:S(2)}) collective-permute-start(bf16[256,1536]{1,0:T(8,128)(2,1)S(1)} %get-tuple-element.148), channel_id=1, source_target_pairs={{0,1},{1,2},{2,3},{3,0},{4,5},{5,6},{6,7},{7,4},{8,9},{9,10},{10,1... | collective-permute-start | bytes 2359304 | tf_op jit(solution)/shard_map/ppermute | solution.py:289
  744.3 66.7 %collective-permute-start.22 = (bf16[256,1536]{1,0:T(8,128)(2,1)}, bf16[256,1536]{1,0:T(8,128)(2,1)}, u32[]{:S(2)}, u32[]{:S(2)}) collective-permute-start(bf16[256,1536]{1,0:T(8,128)(2,1)} %get-tuple-element.150), channel_id=1, source_target_pairs={{0,2},{1,3},{2,0},{3,1},{4,6},{5,7},{6,4},{7,5},{8,10},{9,11},{10,... | collective-permute-start | bytes 2359304 | tf_op jit(solution)/shard_map/ppermute | solution.py:289
  746.8 102.5 %collective-permute-start.23 = (bf16[256,1536]{1,0:T(8,128)(2,1)}, bf16[256,1536]{1,0:T(8,128)(2,1)}, u32[]{:S(2)}, u32[]{:S(2)}) collective-permute-start(bf16[256,1536]{1,0:T(8,128)(2,1)} %get-tuple-element.149), channel_id=1, source_target_pairs={{0,3},{1,0},{2,1},{3,2},{4,7},{5,4},{6,5},{7,6},{8,11},{9,8},{10,9... | collective-permute-start | bytes 2359304 | tf_op jit(solution)/shard_map/ppermute | solution.py:289
  759.4 117.8 %collective-permute-start.27 = (bf16[256,1536]{1,0:T(8,128)(2,1)}, bf16[256,1536]{1,0:T(8,128)(2,1)}, u32[]{:S(2)}, u32[]{:S(2)}) collective-permute-start(bf16[256,1536]{1,0:T(8,128)(2,1)} %get-tuple-element.145), channel_id=1, source_target_pairs={{0,1},{1,2},{2,3},{3,0},{4,5},{5,6},{6,7},{7,4},{8,9},{9,10},{10,1... | collective-permute-start | bytes 2359304 | tf_op jit(solution)/shard_map/ppermute | solution.py:289
  759.7 134.3 %collective-permute-start.28 = (bf16[256,1536]{1,0:T(8,128)(2,1)S(1)}, bf16[256,1536]{1,0:T(8,128)(2,1)}, u32[]{:S(2)}, u32[]{:S(2)}) collective-permute-start(bf16[256,1536]{1,0:T(8,128)(2,1)S(1)} %get-tuple-element.147), channel_id=1, source_target_pairs={{0,2},{1,3},{2,0},{3,1},{4,6},{5,7},{6,4},{7,5},{8,10},{9,11},{10,... | collective-permute-start | bytes 2359304 | tf_op jit(solution)/shard_map/ppermute | solution.py:289
  762.0 137.9 %collective-permute-start.29 = (bf16[256,1536]{1,0:T(8,128)(2,1)S(1)}, bf16[256,1536]{1,0:T(8,128)(2,1)}, u32[]{:S(2)}, u32[]{:S(2)}) collective-permute-start(bf16[256,1536]{1,0:T(8,128)(2,1)S(1)} %get-tuple-element.146), channel_id=1, source_target_pairs={{0,3},{1,0},{2,1},{3,2},{4,7},{5,4},{6,5},{7,6},{8,11},{9,8},{10,9... | collective-permute-start | bytes 2359304 | tf_op jit(solution)/shard_map/ppermute | solution.py:289
  811.0 97.2 %collective-permute-start.41 = (bf16[128,1536]{1,0:T(8,128)(2,1)S(1)}, bf16[128,1536]{1,0:T(8,128)(2,1)S(1)}, u32[]{:S(2)}, u32[]{:S(2)}) collective-permute-start(bf16[128,1536]{1,0:T(8,128)(2,1)S(1)} %get-tuple-element.151), channel_id=1, source_target_pairs={{0,3},{1,0},{2,1},{3,2},{4,7},{5,4},{6,5},{7,6},{8,11},{9,8},{10,9... | collective-permute-start | bytes 1179656 | tf_op jit(solution)/shard_map/ppermute | solution.py:289
  849.3 58.9 %collective-permute-start.42 = (bf16[128,1536]{1,0:T(8,128)(2,1)S(1)}, bf16[128,1536]{1,0:T(8,128)(2,1)S(1)}, u32[]{:S(2)}, u32[]{:S(2)}) collective-permute-start(bf16[128,1536]{1,0:T(8,128)(2,1)S(1)} %get-tuple-element.153), channel_id=1, source_target_pairs={{0,2},{1,3},{2,0},{3,1},{4,6},{5,7},{6,4},{7,5},{8,10},{9,11},{10,... | collective-permute-start | bytes 1179656 | tf_op jit(solution)/shard_map/ppermute | solution.py:289
  877.2 33.6 %collective-permute-start.43 = (bf16[128,1536]{1,0:T(8,128)(2,1)S(1)}, bf16[128,1536]{1,0:T(8,128)(2,1)S(1)}, u32[]{:S(2)}, u32[]{:S(2)}) collective-permute-start(bf16[128,1536]{1,0:T(8,128)(2,1)S(1)} %get-tuple-element.152), channel_id=1, source_target_pairs={{0,1},{1,2},{2,3},{3,0},{4,5},{5,6},{6,7},{7,4},{8,9},{9,10},{10,1... | collective-permute-start | bytes 1179656 | tf_op jit(solution)/shard_map/ppermute | solution.py:289
  904.3 7.6 collective-permute-start.30
  917.2 9.5 collective-permute-start.33
  926.6 25.8 %collective-permute-start.34 = (f32[3096]{0:T(1024)S(1)}, f32[3096]{0:T(1024)S(1)}, u32[]{:S(2)}, u32[]{:S(2)}) collective-permute-start(f32[3096]{0:T(1024)S(1)} %add.337), channel_id=1, source_target_pairs={{0,2},{1,3},{2,0},{3,1},{4,6},{5,7},{6,4},{7,5},{8,10},{9,11},{10,... | collective-permute-start | bytes 37160 | tf_op jit(solution)/shard_map/ppermute | solution.py:250
  945.0 15.5 %collective-permute-start.38 = (bf16[192,2048]{1,0:T(8,128)(2,1)S(1)}, bf16[192,2048]{1,0:T(8,128)(2,1)S(1)}, u32[]{:S(2)}, u32[]{:S(2)}) collective-permute-start(bf16[192,2048]{1,0:T(8,128)(2,1)S(1)} %bitcast.184), channel_id=1, source_target_pairs={{0,3},{1,0},{2,1},{3,2},{4,7},{5,4},{6,5},{7,6},{8,11},{9,8},{10,9... | collective-permute-start | bytes 2359304 | tf_op jit(solution)/shard_map/ppermute | solution.py:289
  945.3 52.8 %collective-permute-start.39 = (bf16[192,2048]{1,0:T(8,128)(2,1)S(1)}, bf16[192,2048]{1,0:T(8,128)(2,1)S(1)}, u32[]{:S(2)}, u32[]{:S(2)}) collective-permute-start(bf16[192,2048]{1,0:T(8,128)(2,1)S(1)} %bitcast.185), channel_id=1, source_target_pairs={{0,2},{1,3},{2,0},{3,1},{4,6},{5,7},{6,4},{7,5},{8,10},{9,11},{10,... | collective-permute-start | bytes 2359304 | tf_op jit(solution)/shard_map/ppermute | solution.py:289
  947.9 67.0 %collective-permute-start.40 = (bf16[192,2048]{1,0:T(8,128)(2,1)S(1)}, bf16[192,2048]{1,0:T(8,128)(2,1)S(1)}, u32[]{:S(2)}, u32[]{:S(2)}) collective-permute-start(bf16[192,2048]{1,0:T(8,128)(2,1)S(1)} %bitcast.186), channel_id=1, source_target_pairs={{0,1},{1,2},{2,3},{3,0},{4,5},{5,6},{6,7},{7,4},{8,9},{9,10},{10,1... | collective-permute-start | bytes 2359304 | tf_op jit(solution)/shard_map/ppermute | solution.py:289
  1018.2 6.2 collective-permute-start.35
  1018.3 10.0 collective-permute-start.36
  1021.6 9.8 collective-permute-start.37
  (39 other events, 1011.0 us)
Sparse Core Ops, SparseCore 0:
  10.1 37.0 all-gather.4
  63.7 92.3 all-gather.8
  162.2 128.0 all-gather.6
  473.3 91.2 reduce-scatter.3
  568.0 156.2 reduce-scatter.5
  732.1 74.5 reduce-scatter.7
